TPU v7x, 256 devices: a whole 4x4x8 slice. The times are simulated.
256 devices in a mesh: dp: 16 (over x, y), expert: 16 (over z, core).
Axes of the slice: x: 4, y: 4, z: 8, core: 2. Of those that a mesh axis runs over, the one named last changes fastest.
Arguments:
- cotangent: bfloat16 [32768, 4096], P(('dp', 'expert')), may hold values from -6 to 6
- hidden: bfloat16 [16, 16, 256, 768], P('dp', 'expert'), may hold values from -6 to 6
- down_matrix: bfloat16 [16, 4096, 768], P('expert'), may hold values from -0.21875 to 0.21875
- adapter_in: bfloat16 [2, 128, 768], replicated, may hold values from -0.21875 to 0.21875
- adapter_out: bfloat16 [2, 4096, 128], replicated, may hold values from -0.5 to 0.5
- probs: bfloat16 [32768, 8], P(('dp', 'expert')), may hold values from 0.019897461 to 0.5
- routes: int32 [32768, 8], P(('dp', 'expert')), may hold values from 0 to 127, as said below
- token_loop: int32 [32768], P(('dp', 'expert')), may hold values from 0 to 1
Outputs:
- hidden_gradient: bfloat16 [16, 16, 256, 768], P('dp', 'expert')
- down_matrix_gradient: float32 [16, 4096, 768], P('expert', 'dp')
- combine_weight_gradient: float32 [32768, 8], P(('dp', 'expert'))
- adapter_in_gradient: float32 [2, 128, 768], P(None, 'expert', 'dp')
- adapter_out_gradient: float32 [2, 4096, 128], P(None, 'dp', 'expert')
Inputs may be any that keep to these rules, and one draw needn't show every extreme that they name: `routes`: each row names 8 different experts. In the 128 rows of one device every expert below 16 is named by 4 to 16 rows, and within each index of dp one such expert is named by exactly 16 rows of every device.
All inputs are finite; a program needn't handle non-finite values.
Results may differ from a plain program's by a relative error of at most 0.0049.
Values may be sent and summed in bfloat16 or wider, within the bound.
A program may use at most 128 MiB of HBM per device.

v0:
```python
import jax
import jax.numpy as jnp
from jax import lax
from jax.sharding import PartitionSpec as P


def route_slots(routes, owner_devices, slot_capacity):
    experts = jnp.arange(owner_devices, dtype=jnp.int32)
    named_count = jnp.sum((routes[:, :, None] == experts[None, None, :]).astype(jnp.int32), axis=1)
    before = jnp.cumsum(named_count, axis=0) - named_count
    in_window = routes < owner_devices
    target = jnp.where(in_window, routes, 0)
    column = jnp.take_along_axis(before, target, axis=1)
    slot_index = jnp.where(
        in_window, target * slot_capacity + column, owner_devices * slot_capacity
    )
    return (in_window, slot_index)


def on_device(cotangent, hidden, down_matrix, adapter_in, adapter_out, probs, routes, token_loop):
    owner_devices = lax.axis_size("expert")
    dp_size = lax.axis_size("dp")
    tok_count, model_width = cotangent.shape
    loop_number, adapter_rank_size, hidden_unit_count = adapter_in.shape
    route_count = routes.shape[1]
    slot_capacity = hidden.shape[2] // owner_devices
    slot_count = owner_devices * slot_capacity
    in_window, slot_index = route_slots(routes, owner_devices, slot_capacity)
    token_index = jnp.broadcast_to(
        jnp.arange(tok_count, dtype=jnp.int32)[:, None], slot_index.shape
    )
    slot_token = (
        jnp.full((slot_count,), tok_count, jnp.int32)
        .at[slot_index.reshape(-1)]
        .set(token_index.reshape(-1), mode="drop")
    )
    slot_weight = (
        jnp.zeros((slot_count,), jnp.float32)
        .at[slot_index.reshape(-1)]
        .set(probs.astype(jnp.float32).reshape(-1), mode="drop")
    )
    loop_mask = (token_loop[:, None] == jnp.arange(loop_number, dtype=jnp.int32)[None, :]).astype(
        jnp.float32
    )
    padded_dy = jnp.concatenate([cotangent, jnp.zeros((1, model_width), jnp.bfloat16)], axis=0)
    padded_mask = jnp.concatenate([loop_mask, jnp.zeros((1, loop_number), jnp.float32)], axis=0)
    send_dy = padded_dy[slot_token].reshape(owner_devices, slot_capacity, model_width)
    send_mix = (
        (slot_weight[:, None] * padded_mask[slot_token])
        .astype(jnp.bfloat16)
        .reshape(owner_devices, slot_capacity, loop_number)
    )
    got_dy, got_mix = (
        lax.all_to_all(send_dy, "expert", split_axis=0, concat_axis=0, tiled=True),
        lax.all_to_all(send_mix, "expert", split_axis=0, concat_axis=0, tiled=True),
    )
    received_output_gradient = got_dy.reshape(slot_count, model_width)
    weight_mix = got_mix.reshape(slot_count, loop_number).astype(jnp.float32)
    arrived_mask = (weight_mix > 0.0).astype(jnp.float32)
    every_loop = jnp.einsum(
        "ct,jtg->cjg", received_output_gradient, adapter_out, preferred_element_type=jnp.float32
    )
    projected = jnp.sum(every_loop * arrived_mask[:, :, None], axis=1).astype(jnp.bfloat16)
    weight_slot = jnp.sum(weight_mix, axis=1)
    hidden_row_block = hidden.reshape(slot_count, hidden_unit_count)
    adapter_flattened = adapter_in.reshape(loop_number * adapter_rank_size, hidden_unit_count)
    masked_projection = (
        (projected[:, None, :].astype(jnp.float32) * arrived_mask[:, :, None])
        .astype(jnp.bfloat16)
        .reshape(slot_count, loop_number * adapter_rank_size)
    )
    input_gradient = jnp.dot(
        received_output_gradient, down_matrix[0], preferred_element_type=jnp.float32
    ) + jnp.dot(masked_projection, adapter_flattened, preferred_element_type=jnp.float32)
    hidden_gradient = (weight_slot[:, None] * input_gradient).astype(jnp.bfloat16)
    grad_mix = jnp.sum(hidden_row_block.astype(jnp.float32) * input_gradient, axis=1)
    scaled = (weight_slot[:, None] * received_output_gradient.astype(jnp.float32)).astype(
        jnp.bfloat16
    )
    weighted_proj = (weight_slot[:, None] * projected.astype(jnp.float32)).astype(jnp.bfloat16)
    masked_weighted = (
        (weighted_proj[:, None, :].astype(jnp.float32) * arrived_mask[:, :, None])
        .astype(jnp.bfloat16)
        .reshape(slot_count, loop_number * adapter_rank_size)
    )
    grad_a = lax.dot_general(
        masked_weighted,
        hidden_row_block,
        (((0,), (0,)), ((), ())),
        preferred_element_type=jnp.float32,
    ).reshape(loop_number, adapter_rank_size, hidden_unit_count)
    down_rank = lax.dot_general(
        hidden_row_block,
        adapter_flattened,
        (((1,), (1,)), ((), ())),
        preferred_element_type=jnp.float32,
    ).reshape(slot_count, loop_number, adapter_rank_size)
    weighted_down = weight_slot[:, None] * jnp.sum(down_rank * arrived_mask[:, :, None], axis=1)
    back_mix, back_down = (
        lax.all_to_all(
            grad_mix.reshape(owner_devices, slot_capacity),
            "expert",
            split_axis=0,
            concat_axis=0,
            tiled=True,
        ),
        lax.all_to_all(
            weighted_down.reshape(owner_devices, slot_capacity, adapter_rank_size),
            "expert",
            split_axis=0,
            concat_axis=0,
            tiled=True,
        ),
    )
    position = jnp.minimum(slot_index, slot_count - 1)
    combine_weight_gradient = jnp.where(in_window, back_mix.reshape(slot_count)[position], 0.0)
    pulled = back_down.reshape(slot_count, adapter_rank_size)[position.reshape(-1)].reshape(
        tok_count, route_count, adapter_rank_size
    )
    summed = jnp.sum(jnp.where(in_window[:, :, None], pulled, 0.0), axis=1).astype(jnp.bfloat16)
    masked_sum = (summed[:, None, :].astype(jnp.float32) * loop_mask[:, :, None]).astype(
        jnp.bfloat16
    )
    grad_b = jnp.einsum("td,tlk->ldk", cotangent, masked_sum, preferred_element_type=jnp.float32)
    part_rows = model_width // dp_size
    down_matrix_gradient = lax.psum_scatter(
        lax.dot_general(
            scaled, hidden_row_block, (((0,), (0,)), ((), ())), preferred_element_type=jnp.float32
        ),
        "dp",
        scatter_dimension=0,
        tiled=True,
    )
    part_a, part_b = (
        lax.psum_scatter(grad_a, "dp", scatter_dimension=2, tiled=True),
        lax.psum_scatter(grad_b, "dp", scatter_dimension=1, tiled=True),
    )
    done_a, done_b = (
        lax.psum_scatter(part_a, "expert", scatter_dimension=1, tiled=True),
        lax.psum_scatter(part_b, "expert", scatter_dimension=2, tiled=True),
    )
    return (
        hidden_gradient.reshape(hidden.shape),
        down_matrix_gradient.reshape(1, part_rows, hidden_unit_count),
        combine_weight_gradient,
        done_a,
        done_b,
    )


def solution(mesh):
    return jax.shard_map(
        on_device,
        mesh=mesh,
        in_specs=(
            P(("dp", "expert"), None),
            P("dp", "expert", None, None),
            P("expert", None, None),
            P(),
            P(),
            P(("dp", "expert"), None),
            P(("dp", "expert"), None),
            P(("dp", "expert")),
        ),
        out_specs=(
            P("dp", "expert", None, None),
            P("expert", "dp", None),
            P(("dp", "expert"), None),
            P(None, "expert", "dp"),
            P(None, "dp", "expert"),
        ),
        check_vma=False,
    )
```

profile of v0, /device:TPU:1, one launch (start us, length us, event | category | flops | bytes accessed | tf_op | source)
XLA Modules:
  0.0 397.7 jit_solution(2618016104132179102)
XLA Ops:
  7.2 0.9 convert_reduce_fusion
  8.0 0.8 copy.68
  9.9 0.8 copy.72
  11.0 7.1 %gather_fusion.4 = s32[1024]{0:T(1024)S(1)} fusion(s32[128,16]{1,0:T(8,128)S(1)} %sub.3, s32[1024]{0:T(1024)S(1)} %reshape.270), kind=kCustom, calls=%fused_computation.4 | custom fusion | bytes 16384 | tf_op jit(solution)/shard_map/jit(take_along_axis)/gather | solution.py:13
  18.4 4.3 %scatter_custom_fusion = f32[256]{0:T(256)S(1)} fusion(s32[1024]{0:T(1024)S(1)} %bitcast.70, f32[1024]{0:T(1024)S(1)} %reshape.280, f32[]{:T(128)} %constant.10.clone.1), kind=kCustom, calls=%fused_computation.64 | custom fusion | bytes 1028 | tf_op jit(solution)/shard_map/scatter | solution.py:40
  22.7 4.3 %scatter_custom_fusion.1 = s32[256]{0:T(256)S(1)} fusion(s32[1024]{0:T(1024)S(1)} %bitcast.71, s32[1024]{0:T(1024)S(1)} %reshape.288, s32[]{:T(128)} %constant.16.clone.1), kind=kCustom, calls=%fused_computation.62 | custom fusion | bytes 1028 | tf_op jit(solution)/shard_map/scatter | solution.py:35
  28.6 10.0 %all-to-all-start = ((bf16[16,16,2]{1,2,0:T(2,128)(2,1)}), bf16[16,16,2]{1,2,0:T(2,128)(2,1)S(1)}, u32[]{:S(2)}, u32[]{:S(2)}) async-start(bf16[16,16,2]{1,2,0:T(2,128)(2,1)} %copy.75), calls=%async_computation | async-start | bytes 16384 | tf_op jit(solution)/shard_map/all_to_all | solution.py:55
  38.7 6.9 %all-to-all-done = bf16[16,16,2]{1,2,0:T(2,128)(2,1)S(1)} async-done(((bf16[16,16,2]{1,2,0:T(2,128)(2,1)}), bf16[16,16,2]{1,2,0:T(2,128)(2,1)S(1)}, u32[]{:S(2)}, u32[]{:S(2)}) %all-to-all-start) | async-done | bytes 1056 | tf_op jit(solution)/shard_map/all_to_all | solution.py:55
  46.7 4.0 all-to-all-start.3
  50.8 9.1 %all-to-all-done.3 = f32[16,16,128]{2,1,0:T(8,128)S(1)} async-done(((f32[16,16,128]{2,1,0:T(8,128)}), f32[16,16,128]{2,1,0:T(8,128)S(1)}, u32[]{:S(2)}, u32[]{:S(2)}) %all-to-all-start.3) | async-done | bytes 131104 | tf_op jit(solution)/shard_map/all_to_all | solution.py:107
  59.9 4.0 %gather_fusion.3 = f32[1024,128]{1,0:T(8,128)} fusion(f32[256,128]{1,0:T(8,128)S(1)} %bitcast.64, s32[1024]{0:T(1024)S(1)} %broadcast_clamp_fusion), kind=kCustom, calls=%fused_computation.3 | custom fusion | bytes 1052672 | tf_op jit(solution)/shard_map/gather | solution.py:117
  63.9 1.3 fusion.6
  65.3 2.6 convolution_bitcast_fusion
  68.0 1.3 concatenate.7
  69.3 3.2 gather_fusion.1
  72.5 4.3 %all-to-all-start.1 = ((bf16[16,16,4096]{2,1,0:T(8,128)(2,1)}), bf16[16,16,4096]{2,1,0:T(8,128)(2,1)}, u32[]{:S(2)}, u32[]{:S(2)}) async-start(bf16[16,16,4096]{2,1,0:T(8,128)(2,1)} %bitcast.66), calls=%async_computation.1 | async-start | bytes 4194304 | tf_op jit(solution)/shard_map/all_to_all | solution.py:54
  76.9 48.2 %all-to-all-done.1 = bf16[16,16,4096]{2,1,0:T(8,128)(2,1)} async-done(((bf16[16,16,4096]{2,1,0:T(8,128)(2,1)}), bf16[16,16,4096]{2,1,0:T(8,128)(2,1)}, u32[]{:S(2)}, u32[]{:S(2)}) %all-to-all-start.1) | async-done | bytes 2097184 | tf_op jit(solution)/shard_map/all_to_all | solution.py:54
  125.1 2.4 fusion.3
  127.9 1.2 fusion.9
  129.2 3.5 multiply_convert_fusion
  132.7 13.5 %reduce-scatter.9.cloned.1.call-done = f32[2,256,128]{1,2,0:T(8,128)} async-done(((f32[2,4096,128]{1,2,0:T(8,128)}), f32[2,256,128]{1,2,0:T(8,128)}) %reduce-scatter.9.cloned.1.call-update) | async-done | bytes 262160 | tf_op jit(solution)/shard_map/reduce_scatter | solution.py:136
  146.4 8.1 %fusion.11 = f32[4096,768]{1,0:T(8,128)} fusion(bf16[256,4096]{1,0:T(8,128)(2,1)} %bitcast.65, bf16[1,1,256,768]{3,2,1,0:T(8,128)(2,1)S(1)} %copy-done.3), kind=kOutput, calls=%fused_computation.26 | convolution fusion | flops 1610612736 | bytes 15073280 | tf_op jit(solution)/shard_map/dot_general | solution.py:127
  154.6 5.2 %fusion = f32[256,768]{1,0:T(8,128)S(1)} fusion(bf16[256,4096]{1,0:T(8,128)(2,1)} %bitcast.4, bf16[1,4096,768]{2,1,0:T(8,128)(2,1)} %param.10), kind=kOutput, calls=%fused_computation.7 | convolution fusion | flops 1610612736 | bytes 9175040 | tf_op jit(solution)/shard_map/dot_general | solution.py:72
  159.9 1.2 multiply_reduce_fusion
  161.8 9.5 %all-to-all-start.2 = ((f32[16,1,16]{2,1,0:T(1,128)}), f32[16,1,16]{2,1,0:T(1,128)S(1)}, u32[]{:S(2)}, u32[]{:S(2)}) async-start(f32[16,1,16]{2,1,0:T(1,128)} %all_to_all.17), calls=%async_computation.3 | async-start | bytes 16384 | tf_op jit(solution)/shard_map/all_to_all | solution.py:100
  172.5 5.7 %all-to-all-done.2 = f32[16,1,16]{2,1,0:T(1,128)S(1)} async-done(((f32[16,1,16]{2,1,0:T(1,128)}), f32[16,1,16]{2,1,0:T(1,128)S(1)}, u32[]{:S(2)}, u32[]{:S(2)}) %all-to-all-start.2) | async-done | bytes 1056 | tf_op jit(solution)/shard_map/all_to_all | solution.py:100
  179.5 6.8 %gather_fusion.2 = f32[1024]{0:T(1024)S(1)} fusion(f32[256]{0:T(256)S(1)} %reshape.231, s32[1024]{0:T(1024)S(1)} %broadcast_clamp_fusion.1), kind=kCustom, calls=%fused_computation.2 | custom fusion | bytes 12288 | tf_op jit(solution)/shard_map/gather | solution.py:116
  187.1 40.7 %reduce-scatter.7.cloned.1.call-done = f32[2,128,48]{1,2,0:T(8,128)} async-done(((f32[2,128,768]{1,2,0:T(8,128)}), f32[2,128,48]{1,2,0:T(8,128)}) %reduce-scatter.7.cloned.1.call-update) | async-done | bytes 49168 | tf_op jit(solution)/shard_map/reduce_scatter | solution.py:135
  227.8 0.9 copy.79
  228.7 46.3 %all-reduce.2 = f32[2,128,48]{2,0,1:T(2,128)S(1)} all-reduce(f32[2,128,48]{2,0,1:T(2,128)S(1)} %copy.79), channel_id=4, replica_groups=mesh['dp'=16,'expert'=16] {'expert'}, use_global_device_ids=true, to_apply=%region_9.10.clone | all-reduce | flops 12288 | bytes 98304
  275.7 10.6 %reduce-scatter.11.cloned.1.call-done = f32[2,256,8]{1,2,0:T(8,128)} async-done(((f32[2,256,128]{1,2,0:T(8,128)}), f32[2,256,8]{1,2,0:T(8,128)}) %reduce-scatter.11.cloned.1.call-update) | async-done | bytes 16400 | tf_op jit(solution)/shard_map/reduce_scatter | solution.py:140
  286.3 104.9 %reduce-scatter.5.cloned.1.call-done = f32[256,768]{1,0:T(8,128)} async-done(((f32[4096,768]{1,0:T(8,128)}), f32[256,768]{1,0:T(8,128)}) %reduce-scatter.5.cloned.1.call-update) | async-done | bytes 786448 | tf_op jit(solution)/shard_map/reduce_scatter | solution.py:126
  (71 shorter events, 9.5 us)
Async XLA Ops:
  7.2 118.0 %copy-start = (bf16[2,4096,128]{2,1,0:T(8,128)(2,1)S(1)}, bf16[2,4096,128]{2,1,0:T(8,128)(2,1)}, u32[]{:S(2)}) copy-start(bf16[2,4096,128]{2,1,0:T(8,128)(2,1)} %param.12) | copy-start | bytes 6291460
  18.1 27.6 %copy-start.2 = (bf16[1,1,256,768]{3,2,1,0:T(8,128)(2,1)S(1)}, bf16[1,1,256,768]{3,2,1,0:T(8,128)(2,1)}, u32[]{:S(2)}) copy-start(bf16[1,1,256,768]{3,2,1,0:T(8,128)(2,1)} %param.9) | copy-start | bytes 1179652
  18.1 27.6 %copy-start.4 = (bf16[2,128,768]{2,1,0:T(8,128)(2,1)S(1)}, bf16[2,128,768]{2,1,0:T(8,128)(2,1)}, u32[]{:S(2)}) copy-start(bf16[2,128,768]{2,1,0:T(8,128)(2,1)} %param.11) | copy-start | bytes 1179652
  28.6 16.9 %all-to-all-start = ((bf16[16,16,2]{1,2,0:T(2,128)(2,1)}), bf16[16,16,2]{1,2,0:T(2,128)(2,1)S(1)}, u32[]{:S(2)}, u32[]{:S(2)}) async-start(bf16[16,16,2]{1,2,0:T(2,128)(2,1)} %copy.75), calls=%async_computation | async-start | bytes 16384 | tf_op jit(solution)/shard_map/all_to_all | solution.py:55
  46.7 13.1 %all-to-all-start.3 = ((f32[16,16,128]{2,1,0:T(8,128)}), f32[16,16,128]{2,1,0:T(8,128)S(1)}, u32[]{:S(2)}, u32[]{:S(2)}) async-start(f32[16,16,128]{2,1,0:T(8,128)} %broadcast_multiply_fusion), calls=%async_computation.5 | async-start | bytes 262144 | tf_op jit(solution)/shard_map/all_to_all | solution.py:107
  50.7 95.5 %reduce-scatter.9.cloned.1.call-start = ((), (), s32[]{:S(2)}) async-start(), calls=%async_computation.10 | async-start | bytes 4456448 | tf_op jit(solution)/shard_map/reduce_scatter | solution.py:136
  59.9 5.4 %copy-start.1 = (bf16[128,4096]{1,0:T(8,128)(2,1)S(1)}, bf16[128,4096]{1,0:T(8,128)(2,1)}, u32[]{:S(2)}) copy-start(bf16[128,4096]{1,0:T(8,128)(2,1)} %param.8) | copy-start | bytes 3145732
  72.5 52.7 %all-to-all-start.1 = ((bf16[16,16,4096]{2,1,0:T(8,128)(2,1)}), bf16[16,16,4096]{2,1,0:T(8,128)(2,1)}, u32[]{:S(2)}, u32[]{:S(2)}) async-start(bf16[16,16,4096]{2,1,0:T(8,128)(2,1)} %bitcast.66), calls=%async_computation.1 | async-start | bytes 4194304 | tf_op jit(solution)/shard_map/all_to_all | solution.py:54
  76.8 151.0 %reduce-scatter.7.cloned.1.call-start = ((), (), s32[]{:S(2)}) async-start(), calls=%async_computation.9 | async-start | bytes 835584 | tf_op jit(solution)/shard_map/reduce_scatter | solution.py:135
  125.1 2.7 copy-start.3
  129.1 157.2 %reduce-scatter.11.cloned.1.call-start = ((), (), s32[]{:S(2)}) async-start(), calls=%async_computation.11 | async-start | bytes 278528 | tf_op jit(solution)/shard_map/reduce_scatter | solution.py:140
  146.2 245.0 %reduce-scatter.5.cloned.1.call-start = ((), (), s32[]{:S(2)}) async-start(), calls=%async_computation.8 | async-start | bytes 13369344 | tf_op jit(solution)/shard_map/reduce_scatter | solution.py:126
  154.6 5.3 %copy-start.5 = (bf16[2,128,768]{2,1,0:T(8,128)(2,1)S(1)}, bf16[2,128,768]{2,1,0:T(8,128)(2,1)}, u32[]{:S(2)}) copy-start(bf16[2,128,768]{2,1,0:T(8,128)(2,1)} %param.11) | copy-start | bytes 1179652
  159.9 11.4 %copy-start.6 = (u32[256]{0:T(256)S(1)}, u32[256]{0:T(256)}, u32[]{:S(2)}) copy-start(u32[256]{0:T(256)} %constant.66) | copy-start | bytes 3076
  161.8 16.4 %all-to-all-start.2 = ((f32[16,1,16]{2,1,0:T(1,128)}), f32[16,1,16]{2,1,0:T(1,128)S(1)}, u32[]{:S(2)}, u32[]{:S(2)}) async-start(f32[16,1,16]{2,1,0:T(1,128)} %all_to_all.17), calls=%async_computation.3 | async-start | bytes 16384 | tf_op jit(solution)/shard_map/all_to_all | solution.py:100
Sparse Core Ops, SparseCore 0:
  68.1 78.0 reduce-scatter.8
  149.6 78.1 reduce-scatter.6
  230.9 55.3 reduce-scatter.10
  290.5 100.6 reduce-scatter.4
where the time goes:
time: 398 us
  waiting for transfers between devices  240 us (60%)
  blocking collectives  46.3 us (12%)
  local copies, waits for them, and re-layouts  39.6 us (10%)
  starting transfers between devices  28.1 us (7%)
  matrix products  21 us (5%)
  between operations  14.8 us (4%)
  other arithmetic  8.33 us (2%)
    reduce_scatter x1, waiting for transfers between devices, on_device(): lax.psum_scatter(lax.dot_general(scaled, hidden_row_block, (((0,), (0,)),...  105 us
    all_to_all x1, waiting for transfers between devices, on_device(): lax.all_to_all(send_dy, 'expert', split_axis=0, concat_axis=0, tiled=True)  48.2 us
    unnamed x1, blocking collectives  46.3 us
    reduce_scatter x1, waiting for transfers between devices, on_device(): lax.psum_scatter(grad_a, 'dp', scatter_dimension=2, tiled=True)  40.7 us
    reduce_scatter x1, waiting for transfers between devices, on_device(): lax.psum_scatter(grad_b, 'dp', scatter_dimension=1, tiled=True)  13.5 us
    reduce_scatter x1, waiting for transfers between devices, on_device(): lax.psum_scatter(part_b, 'expert', scatter_dimension=2, tiled=True)  10.6 us
    all_to_all x1, starting transfers between devices, on_device(): lax.all_to_all(send_mix, 'expert', split_axis=0, concat_axis=0, tiled=True)  9.97 us
    all_to_all x1, starting transfers between devices, on_device(): lax.all_to_all(grad_mix.reshape(owner_devices, slot_capacity), 'expert',...  9.47 us
  transfers between devices with their start and end apart: 8, of which 8 were waited for; matrix products, arithmetic and copies ran while one was open for 9% of the time, Pallas kernels for 0%

commit v1 on v0

v1 whole, which is shorter than its diff:
```python
import functools

import jax
import jax.numpy as jnp
from jax import lax
from jax.experimental import pallas as pl
from jax.experimental.pallas import tpu as pltpu
from jax.sharding import PartitionSpec as P

MESH = pl.DeviceIdType.MESH
F32 = jnp.float32
BF16 = jnp.bfloat16

NX = 4
NY = 4
NE = 16
CAP = 16
TOK = 128
SLOTS = NE * CAP
MODEL = 4096
HID = 768
RANK = 128
EXT = 2 * RANK
ROWS = MODEL // (NX * NY)
ACOL = HID // (NX * NY)

STEPS = ((1, 0, 256), (2, 0, 256), (3, 0, 256), (0, 0, 128), (0, 128, 128))
NS = len(STEPS)


def rcopy(src, dst, send, recv, dev):
    return pltpu.make_async_remote_copy(
        src_ref=src, dst_ref=dst, send_sem=send, recv_sem=recv, device_id=dev, device_id_type=MESH
    )


def dot(a, b):
    return jnp.dot(a, b, preferred_element_type=F32)


def kernel(cot_h, hid_h, w_h, ain_h, aout_h, probs_ref, routes_ref, loop_ref, *refs):
    hg_ref, dw_ref, cwg_ref, ga_ref, gb_ref = refs[:5]
    (cot, aout, ain, wm, hx, dx, aperm, sbuf, mbuf, acc, sel) = refs[5:16]
    (msend, mrecv, q1s, q1r, q2s, q2r, rzs, rzr, xs_, xr_, gzs, gzr, ps, pr, own) = refs[16:31]
    dys = refs[31 : 31 + NS]
    dyr = refs[31 + NS : 31 + 2 * NS]
    tsd = refs[31 + 2 * NS : 31 + 3 * NS]
    trv = refs[31 + 3 * NS : 31 + 4 * NS]
    (lsem, dy_s, dy_r, m_s, m_r, x_s, x_r, y_s, y_r, z_s, z_r) = refs[31 + 4 * NS :]

    dp = lax.axis_index("dp")
    e = lax.axis_index("expert")
    x = dp // NY
    y = lax.rem(dp, NY)

    def zdev(p):
        return (dp, p)

    def xdev(p):
        return (p * NY + y, e)

    def ydev(p):
        return (x * NY + p, e)

    loads = [
        pltpu.make_async_copy(cot_h, cot, lsem.at[0]),
        pltpu.make_async_copy(hid_h, hx.at[x], lsem.at[1]),
        pltpu.make_async_copy(aout_h, aout, lsem.at[2]),
        pltpu.make_async_copy(ain_h, ain, lsem.at[3]),
        pltpu.make_async_copy(w_h, wm, lsem.at[4]),
    ]
    for one in loads:
        one.start()

    barrier = pltpu.get_barrier_semaphore()

    def greet_z(k, c):
        pl.semaphore_signal(barrier, inc=1, device_id=zdev(lax.rem(e + k, NE)), device_id_type=MESH)
        return c

    lax.fori_loop(1, NE, greet_z, 0)
    for k in range(1, NX):
        pl.semaphore_signal(barrier, inc=1, device_id=xdev(lax.rem(x + k, NX)), device_id_type=MESH)
        pl.semaphore_signal(barrier, inc=1, device_id=ydev(lax.rem(y + k, NY)), device_id_type=MESH)

    routes = routes_ref[...]
    probs = probs_ref[...].astype(F32)
    expert_id = lax.broadcasted_iota(jnp.int32, (NE, TOK), 0)
    named = jnp.zeros((NE, TOK), F32)
    weight = jnp.zeros((NE, TOK), F32)
    for k in range(8):
        hit = (routes[k : k + 1, :] == expert_id).astype(F32)
        named = named + hit
        weight = weight + hit * probs[k : k + 1, :]
    row = lax.broadcasted_iota(jnp.int32, (TOK, TOK), 0)
    col = lax.broadcasted_iota(jnp.int32, (TOK, TOK), 1)
    before = dot(named.astype(BF16), (row < col).astype(F32).astype(BF16))
    before = jnp.where(named > 0.5, before, -1.0)
    place = lax.broadcasted_iota(jnp.int32, (NE, CAP, TOK), 1).astype(F32)
    pick3 = (jnp.broadcast_to(before[:, None, :], (NE, CAP, TOK)) == place).astype(F32)
    pickw = (pick3 * weight[:, None, :]).reshape(SLOTS, TOK)
    pick = pick3.reshape(SLOTS, TOK)
    sel[...] = pick
    second = (loop_ref[...] == 1).astype(F32)
    w1 = jnp.sum(pickw * second, axis=1, keepdims=True)
    w0 = jnp.sum(pickw * (1.0 - second), axis=1, keepdims=True)
    lane = lax.broadcasted_iota(jnp.int32, (SLOTS, RANK), 1)
    mbuf[:, RANK:] = jnp.where(lane >= RANK // 2, w1, w0).astype(BF16)

    def block_of(j):
        off, start, width = STEPS[j]
        return lax.rem(y + off, NY), start, width

    def fill(j):
        yj, start, width = block_of(j)
        picked = sel[...].astype(BF16)

        def one(q, c):
            at = pl.multiple_of((NY * q + yj) * ROWS + start, 128)
            dys[j][q] = dot(picked, cot[:, pl.ds(at, width)]).astype(BF16)
            return c

        lax.fori_loop(0, NX, one, 0)
        mine = pl.ds(pl.multiple_of(e * CAP, CAP), CAP)
        dyr[j][:, mine, :] = dys[j][:, mine, :]

    def blk(p):
        return pl.ds(pl.multiple_of(p * CAP, CAP), CAP)

    def z_each(make):
        def one(k, c):
            make(lax.rem(e + k, NE))
            return c

        lax.fori_loop(1, NE, one, 0)

    def dy_copy(j, p, s):
        return rcopy(
            dys[j].at[:, blk(p), :], dyr[j].at[:, blk(s), :], dy_s.at[j, p], dy_r.at[j, s], zdev(p)
        )

    def meta_copy(p, s):
        return rcopy(mbuf.at[blk(p), :], msend.at[blk(s), :], m_s.at[p], m_r.at[s], zdev(p))

    def h_copy(p, s):
        return rcopy(hx.at[s], hx.at[s], x_s.at[0, p], x_r.at[0, s], xdev(p))

    def d_copy(p, s):
        return rcopy(dx.at[s], dx.at[s], x_s.at[1, p], x_r.at[1, s], xdev(p))

    def q1_copy(p, s):
        return rcopy(q1s.at[p], q1r.at[s], x_s.at[2, p], x_r.at[2, s], xdev(p))

    def t_copy(j, p, s):
        return rcopy(tsd[j].at[p], trv[j].at[s], x_s.at[3 + j, p], x_r.at[3 + j, s], xdev(p))

    def q2_copy(p, s):
        return rcopy(q2s.at[p], q2r.at[s], y_s.at[0, p], y_r.at[0, s], ydev(p))

    def p_copy(j, p):
        return rcopy(ps.at[j], pr.at[j], y_s.at[1, j], y_r.at[1, j], ydev(p))

    def zc(n, src, dst, p, s):
        return rcopy(src.at[p], dst.at[s], z_s.at[n, p], z_r.at[n, s], zdev(p))

    def x_each(make):
        for k in range(1, NX):
            make(lax.rem(x + k, NX))

    def y_each(make):
        for k in range(1, NY):
            make(lax.rem(y + k, NY))

    loads[0].wait()
    fill(0)
    pl.semaphore_wait(barrier, NE - 1 + 2 * 3)
    z_each(lambda p: dy_copy(0, p, e).start())
    loads[1].wait()
    x_each(lambda p: h_copy(p, x).start())

    loads[2].wait()
    picked = sel[...].astype(BF16)
    p0 = dot(cot[...], aout[0]).astype(BF16)
    p1 = dot(cot[...], aout[1]).astype(BF16)
    both = jnp.where(w1 > 0.0, dot(picked, p1), dot(picked, p0))
    mbuf[:, :RANK] = both.astype(BF16)
    mine = blk(e)
    msend[mine, :] = mbuf[mine, :]
    z_each(lambda p: meta_copy(p, e).start())
    for j in range(1, NS):
        fill(j)
        z_each(lambda p: dy_copy(j, p, e).start())

    loads[3].wait()
    for p in range(NE):
        pair = jnp.concatenate(
            [ain[0, 8 * p : 8 * p + 8, :].astype(F32), ain[1, 8 * p : 8 * p + 8, :].astype(F32)], axis=0
        )
        aperm[16 * p : 16 * p + 16, :] = pair.astype(BF16)
    hid = hx[x]
    down = lax.dot_general(hid, aperm[...], (((1,), (1,)), ((), ())), preferred_element_type=F32)

    z_each(lambda s: meta_copy(s, s).wait_recv())
    mix = msend[:, RANK:].astype(F32)
    proj = msend[:, :RANK]
    wfull = mix + pltpu.roll(mix, RANK // 2, 1)
    high = jnp.where(lane >= RANK // 2, mix, 0.0)
    whigh = high + pltpu.roll(high, RANK // 2, 1)
    wlow = wfull - whigh
    mrecv[...] = wfull
    lane2 = lax.broadcasted_iota(jnp.int32, (SLOTS, EXT), 1)
    odd = jnp.bitwise_and(jnp.right_shift(lane2, 3), 1) == 1
    wsel = jnp.where(
        odd, jnp.concatenate([whigh, whigh], axis=1), jnp.concatenate([wlow, wlow], axis=1)
    )
    keep = wsel > 0.0
    dx[x] = jnp.where(keep, down, 0.0).astype(BF16)
    x_each(lambda p: d_copy(p, x).start())
    r_at = lax.broadcasted_iota(jnp.int32, (RANK, EXT), 0)
    n_at = lax.broadcasted_iota(jnp.int32, (RANK, EXT), 1)
    spread = jnp.bitwise_or(
        jnp.left_shift(jnp.right_shift(n_at, 4), 3), jnp.bitwise_and(n_at, 7)
    )
    expand = (spread == r_at).astype(F32).astype(BF16)
    wproj = (wfull * proj.astype(F32)).astype(BF16)
    wpm = jnp.where(keep, dot(wproj, expand), 0.0).astype(BF16)
    projm = jnp.where(keep, dot(proj, expand), 0.0).astype(BF16)
    acc[...] = dot(projm, aperm[...])
    qt = lax.dot_general(hid, wpm, (((0,), (0,)), ((), ())), preferred_element_type=F32)
    for p in range(NX):
        q1s[p] = qt[4 * ACOL * p : 4 * ACOL * (p + 1), :].astype(BF16)
    x_each(lambda p: q1_copy(p, x).start())

    def arrive(j):
        yj, start, width = block_of(j)
        z_each(lambda s: dy_copy(j, s, s).wait_recv())

        def one(q, c):
            wf = mrecv[...]
            if width > RANK:
                wf = jnp.concatenate([wf, wf], axis=1)
            tsd[j][q] = (dyr[j][q].astype(F32) * wf).T.astype(BF16)
            return c

        lax.fori_loop(0, NX, one, 0)
        x_each(lambda p: t_copy(j, p, x).start())
        if j == 0:
            loads[4].wait()

        def two(q, c):
            at = pl.multiple_of((NY * q + yj) * ROWS + start, 128)
            acc[...] += dot(dyr[j][q], wm[pl.ds(at, width), :])
            return c

        lax.fori_loop(0, NX, two, 0)

    def product(j):
        x_each(lambda s: t_copy(j, s, s).wait_recv())
        if j == 0:
            x_each(lambda s: h_copy(s, s).wait_recv())
            x_each(lambda s: d_copy(s, s).wait_recv())
        mine = tsd[j][x]
        main = dot(mine, hx[x])
        extra = dot(mine, dx[x])
        for k in range(1, NX):
            s = lax.rem(x + k, NX)
            main = main + dot(trv[j][s], hx[s])
            extra = extra + dot(trv[j][s], dx[s])
        return main, extra

    def reduce_y(j):
        main, extra = product(j)
        ps[j, :, :HID] = main.astype(BF16)
        ps[j, :, HID:] = extra.astype(BF16)
        p_copy(j, lax.rem(y + STEPS[j][0], NY)).start()

    arrive(0)
    x_each(lambda s: q1_copy(s, s).wait_recv())
    total = q1s[x].astype(F32)
    for k in range(1, NX):
        total = total + q1r[lax.rem(x + k, NX)].astype(F32)
    for p in range(NY):
        q2s[p] = total[ACOL * p : ACOL * (p + 1), :].astype(BF16)
    y_each(lambda p: q2_copy(p, y).start())
    reduce_y(0)

    arrive(1)
    y_each(lambda s: q2_copy(s, s).wait_recv())
    total = q2s[y].astype(F32)
    for k in range(1, NY):
        total = total + q2r[lax.rem(y + k, NY)].astype(F32)
    padded = jnp.concatenate([total, jnp.zeros((RANK - ACOL, EXT), F32)], axis=0)
    rzs[...] = padded.T.astype(BF16).reshape(NE, 16, RANK)
    z_each(lambda p: zc(0, rzs, rzr, p, e).start())
    reduce_y(1)

    arrive(2)
    z_each(lambda s: zc(0, rzs, rzr, s, s).wait_recv())
    rzr[e] = rzs[e]
    total = jnp.sum(rzr[...].astype(F32), axis=0)
    ga_ref[0] = total[:8, :ACOL]
    ga_ref[1] = total[8:, :ACOL]
    reduce_y(2)

    arrive(3)
    arrive(4)
    grad = acc[...]
    wf = mrecv[...]
    mixed = jnp.sum(hx[x].astype(F32) * grad, axis=1, keepdims=True)
    place2 = lax.broadcasted_iota(jnp.int32, (NE, CAP, RANK), 1)
    lane3 = lax.broadcasted_iota(jnp.int32, (NE, CAP, RANK), 2)
    diag = place2 == lane3
    spreadm = jnp.broadcast_to(mixed, (SLOTS, RANK)).reshape(NE, CAP, RANK)
    rows = jnp.sum(jnp.where(diag, spreadm, 0.0), axis=1)
    xs_[...] = jnp.broadcast_to(rows[:, None, :], (NE, 8, RANK))
    z_each(lambda p: zc(1, xs_, xr_, p, e).start())
    hg_ref[...] = (jnp.concatenate([wf] * (HID // RANK), axis=1) * grad).astype(BF16)

    for j in range(3, NS):
        off, start, width = STEPS[j]
        main, extra = product(j)
        if j == 3:
            for k in range(3):
                p_copy(k, k).wait_recv()
        part = slice(start, start + width)
        for k in range(3):
            main = main + pr[k, part, :HID].astype(F32)
            extra = extra + pr[k, part, HID:].astype(F32)
        dw_ref[part, :] = main
        own[part, :] = extra
    gzs[...] = own[...].T.astype(BF16).reshape(NE, 16, ROWS)
    z_each(lambda p: zc(2, gzs, gzr, p, e).start())

    z_each(lambda s: zc(1, xs_, xr_, s, s).wait_recv())
    xr_[e] = xs_[e]
    got = jnp.broadcast_to(xr_[:, 0:1, :], (NE, CAP, RANK))
    column = jnp.sum(jnp.where(diag, got, 0.0), axis=2, keepdims=True)
    per_expert = jnp.sum(sel[...].reshape(NE, CAP, TOK) * column, axis=1)
    for k in range(8):
        hit = routes_ref[k : k + 1, :] == expert_id
        cwg_ref[k : k + 1, :] = jnp.sum(jnp.where(hit, per_expert, 0.0), axis=0, keepdims=True)

    z_each(lambda s: zc(2, gzs, gzr, s, s).wait_recv())
    gzr[e] = gzs[e]
    total = jnp.sum(gzr[...].astype(F32), axis=0)
    gb_ref[0] = total[:8, :]
    gb_ref[1] = total[8:, :]

    for j in range(NS):
        z_each(lambda p: dy_copy(j, p, e).wait_send())
        x_each(lambda p: t_copy(j, p, x).wait_send())
    z_each(lambda p: meta_copy(p, e).wait_send())
    z_each(lambda p: zc(0, rzs, rzr, p, e).wait_send())
    z_each(lambda p: zc(1, xs_, xr_, p, e).wait_send())
    z_each(lambda p: zc(2, gzs, gzr, p, e).wait_send())
    x_each(lambda p: h_copy(p, x).wait_send())
    x_each(lambda p: d_copy(p, x).wait_send())
    x_each(lambda p: q1_copy(p, x).wait_send())
    y_each(lambda p: q2_copy(p, y).wait_send())
    for j in range(3):
        p_copy(j, lax.rem(y + STEPS[j][0], NY)).wait_send()


def on_device(cotangent, hidden, down_matrix, adapter_in, adapter_out, probs, routes, token_loop):
    vmem = pl.BlockSpec(memory_space=pltpu.VMEM)
    anyw = pl.BlockSpec(memory_space=pl.ANY)
    widths = [w for _, _, w in STEPS]
    scratch = [
        pltpu.VMEM((TOK, MODEL), BF16),
        pltpu.VMEM((2, MODEL, RANK), BF16),
        pltpu.VMEM((2, RANK, HID), BF16),
        pltpu.VMEM((MODEL, HID), BF16),
        pltpu.VMEM((NX, SLOTS, HID), BF16),
        pltpu.VMEM((NX, SLOTS, EXT), BF16),
        pltpu.VMEM((EXT, HID), BF16),
        pltpu.VMEM((8, RANK), F32),
        pltpu.VMEM((SLOTS, EXT), BF16),
        pltpu.VMEM((SLOTS, HID), F32),
        pltpu.VMEM((SLOTS, TOK), F32),
        pltpu.VMEM((SLOTS, EXT), BF16),
        pltpu.VMEM((SLOTS, RANK), F32),
        pltpu.VMEM((NX, 4 * ACOL, EXT), BF16),
        pltpu.VMEM((NX, 4 * ACOL, EXT), BF16),
        pltpu.VMEM((NY, ACOL, EXT), BF16),
        pltpu.VMEM((NY, ACOL, EXT), BF16),
        pltpu.VMEM((NE, 16, RANK), BF16),
        pltpu.VMEM((NE, 16, RANK), BF16),
        pltpu.VMEM((NE, 8, RANK), F32),
        pltpu.VMEM((NE, 8, RANK), F32),
        pltpu.VMEM((NE, 16, ROWS), BF16),
        pltpu.VMEM((NE, 16, ROWS), BF16),
        pltpu.VMEM((3, ROWS, HID + EXT), BF16),
        pltpu.VMEM((3, ROWS, HID + EXT), BF16),
        pltpu.VMEM((ROWS, EXT), F32),
    ]
    scratch += [pltpu.VMEM((NX, SLOTS, w), BF16) for w in widths]
    scratch += [pltpu.VMEM((NX, SLOTS, w), BF16) for w in widths]
    scratch += [pltpu.VMEM((NX, w, SLOTS), BF16) for w in widths]
    scratch += [pltpu.VMEM((NX, w, SLOTS), BF16) for w in widths]
    sem = pltpu.SemaphoreType.DMA
    scratch += [
        sem((5,)),
        sem((NS, NE)),
        sem((NS, NE)),
        sem((NE,)),
        sem((NE,)),
        sem((3 + NS, NX)),
        sem((3 + NS, NX)),
        sem((2, NY)),
        sem((2, NY)),
        sem((3, NE)),
        sem((3, NE)),
    ]
    hg, dw, cwg, ga, gb = pl.pallas_call(
        kernel,
        out_shape=(
            jax.ShapeDtypeStruct((SLOTS, HID), BF16),
            jax.ShapeDtypeStruct((ROWS, HID), F32),
            jax.ShapeDtypeStruct((8, TOK), F32),
            jax.ShapeDtypeStruct((2, 8, ACOL), F32),
            jax.ShapeDtypeStruct((2, 8, ROWS), F32),
        ),
        in_specs=[anyw] * 5 + [vmem] * 3,
        out_specs=(vmem,) * 5,
        scratch_shapes=scratch,
        compiler_params=pltpu.CompilerParams(
            collective_id=0, has_side_effects=True, vmem_limit_bytes=56 * 2**20
        ),
        name="backward",
    )(
        cotangent,
        hidden.reshape(SLOTS, HID),
        down_matrix.reshape(MODEL, HID),
        adapter_in,
        adapter_out,
        probs.T,
        routes.T,
        token_loop.reshape(1, TOK),
    )
    return (
        hg.reshape(hidden.shape),
        dw.reshape(1, ROWS, HID),
        cwg.T,
        ga,
        jnp.swapaxes(gb, 1, 2),
    )


def solution(mesh):
    return jax.shard_map(
        on_device,
        mesh=mesh,
        in_specs=(
            P(("dp", "expert"), None),
            P("dp", "expert", None, None),
            P("expert", None, None),
            P(),
            P(),
            P(("dp", "expert"), None),
            P(("dp", "expert"), None),
            P(("dp", "expert")),
        ),
        out_specs=(
            P("dp", "expert", None, None),
            P("expert", "dp", None),
            P(("dp", "expert"), None),
            P(None, "expert", "dp"),
            P(None, "dp", "expert"),
        ),
        check_vma=False,
    )
```

time: 398 us -> 102 us (0.26)
  waiting for transfers between devices: 240 us -> 0 us
  Pallas kernels: 0 us -> 92.8 us
  blocking collectives: 46.3 us -> 0 us
  local copies, waits for them, and re-layouts: 39.6 us -> 7.72 us
  starting transfers between devices: 28.1 us -> 0 us
  matrix products: 21 us -> 0 us
  between operations: 14.8 us -> 0.64 us
  other arithmetic: 8.33 us -> 0 us
    reduce_scatter x4 -> x0, waiting for transfers between devices: 170 us -> none  [the longest x1 105 us: on_device(): lax.psum_scatter(lax.dot_general(scaled, hidden_row_block, (((0,), (0,)),...]
    pallas_call x0 -> x1, Pallas kernels: none -> 92.8 us  [on_device(): pl.pallas_call(kernel, out_shape=(jax.ShapeDtypeStruct((SLOTS, HID), BF16...]
    all_to_all x4 -> x0, waiting for transfers between devices: 69.9 us -> none  [the longest x1 48.2 us: on_device(): lax.all_to_all(send_dy, 'expert', split_axis=0, concat_axis=0, tiled=True)]
    unnamed x1 -> x0, blocking collectives: 46.3 us -> none
    all_to_all x4 -> x0, starting transfers between devices: 27.7 us -> none  [the longest x1 9.97 us: on_device(): lax.all_to_all(send_mix, 'expert', split_axis=0, concat_axis=0, tiled=True)]
    gather x9 -> x0, local copies, waits for them, and re-layouts: 22.2 us -> none  [the longest x3 7.24 us: route_slots(): column = jnp.take_along_axis(before, target, axis=1)]
    dot_general x7 -> x0, matrix products: 21 us -> none  [the longest x1 8.05 us: on_device(): lax.dot_general(scaled, hidden_row_block, (((0,), (0,)), ((), ())), prefe...]
    scatter x2 -> x0, local copies, waits for them, and re-layouts: 8.61 us -> none  [the longest x1 4.3 us: on_device(): slot_weight = jnp.zeros((slot_count,), jnp.float32).at[slot_index.reshape...]
  transfers between devices with their start and end apart: 8 -> 0, of which waited for: 8 -> 0; matrix products, arithmetic and copies ran while one was open for 9% -> 0% of each run, Pallas kernels for 0% -> 0%
where the time goes in v1:
time: 102 us; the launch traced here: 101 us
  Pallas kernels  92.8 us (91%)
  local copies, waits for them, and re-layouts  7.72 us (8%)
    pallas_call x1, Pallas kernels, on_device(): pl.pallas_call(kernel, out_shape=(jax.ShapeDtypeStruct((SLOTS, HID), BF16...  92.8 us
    unnamed x5, local copies, waits for them, and re-layouts  7.72 us

profile of v1, /device:TPU:1, one launch (start us, length us, event | category | flops | bytes accessed | tf_op | source)
XLA Modules:
  0.0 101.2 jit_solution(6065774621960191712)
XLA Ops:
  0.6 92.8 %backward.1 = (bf16[256,768]{1,0:T(8,128)(2,1)}, f32[256,768]{1,0:T(8,128)}, f32[8,128]{1,0:T(8,128)}, f32[2,8,48]{2,1,0:T(8,128)}, f32[2,8,256]{2,1,0:T(8,128)}) custom-call(bf16[128,4096]{1,0:T(8,128)(2,1)} %cot_h.1, bf16[256,768]{1,0:T(8,128)(2,1)} %bitcast.12, bf16[4096,768]{1,0:T(8,128)(2,1)} %bitcast.9, bf16[2,128,768]{2,1,0:T(8,128)(2,1)} %ain_h.1, ...), custom_call_target="tpu_custom_call" | custom-call | tf_op jit(solution)/shard_map/backward/pallas_call | solution.py:414
  93.5 1.8 %copy.18 = bf16[1,1,256,768]{3,2,1,0:T(8,128)(2,1)} copy(bf16[1,1,256,768]{3,2,1,0:T(8,128)(2,1)} %bitcast.11) | data formatting | bytes 786432
  95.2 2.1 %copy.19 = f32[1,256,768]{2,1,0:T(8,128)} copy(f32[1,256,768]{2,1,0:T(8,128)} %bitcast.10) | data formatting | bytes 1572864
  97.3 1.3 %copy.20 = f32[128,8]{0,1:T(8,128)} copy(f32[128,8]{0,1:T(8,128)} %bitcast.15) | data formatting | bytes 8192
  98.6 1.3 %copy.21 = f32[2,8,48]{2,1,0:T(8,128)} copy(f32[2,8,48]{2,1,0:T(8,128)} %get-tuple-element.23) | data formatting | bytes 6144
  99.9 1.3 %copy.22 = f32[2,256,8]{1,2,0:T(8,128)} copy(f32[2,256,8]{1,2,0:T(8,128)} %bitcast.13) | data formatting | bytes 32768

commit v2 on v1

v2 whole, which is shorter than its diff:
```python
import functools

import jax
import jax.numpy as jnp
from jax import lax
from jax.experimental import pallas as pl
from jax.experimental.pallas import tpu as pltpu
from jax.sharding import PartitionSpec as P

MESH = pl.DeviceIdType.MESH
F32 = jnp.float32
BF16 = jnp.bfloat16

NX = 4
NY = 4
NE = 16
CAP = 16
TOK = 128
SLOTS = NE * CAP
MODEL = 4096
HID = 768
RANK = 128
EXT = 2 * RANK
ROWS = MODEL // (NX * NY)
ACOL = HID // (NX * NY)

STEPS = (
    (1, 0, 256),
    (2, 0, 128),
    (2, 128, 128),
    (3, 0, 128),
    (3, 128, 128),
    (0, 0, 128),
    (0, 128, 128),
)
NS = len(STEPS)
NP = sum(1 for off, _, _ in STEPS if off)


def rcopy(src, dst, send, recv, dev):
    return pltpu.make_async_remote_copy(
        src_ref=src, dst_ref=dst, send_sem=send, recv_sem=recv, device_id=dev, device_id_type=MESH
    )


def dot(a, b):
    return jnp.dot(a, b, preferred_element_type=F32)


def dot_t(a, b):
    return lax.dot_general(a, b, (((1,), (1,)), ((), ())), preferred_element_type=F32)


def blk(p):
    return pl.ds(pl.multiple_of(p * CAP, CAP), CAP)


def kernel(cot_h, hid_h, w_h, ain_h, aout_h, probs_ref, routes_ref, loop_ref, *refs):
    hg_ref, dw_ref, cwg_ref, ga_ref, gb_ref = refs[:5]
    (cot, aout, ain, wm, hx, dx, aperm, pbuf, precv, wv, acc, sel) = refs[5:17]
    (mrow, mxr, mxs, q1s, q1r, q2s, q2r, rzs, rzr, xs, xr, gzs, gzr, ps, pr) = refs[17:32]
    dys = refs[32 : 32 + NS]
    dyr = refs[32 + NS : 32 + 2 * NS]
    tsd = refs[32 + 2 * NS : 32 + 3 * NS]
    trv = refs[32 + 3 * NS : 32 + 4 * NS]
    lsem, z_s, z_r, x_s, x_r, y_s, y_r = refs[32 + 4 * NS :]

    dp = lax.axis_index("dp")
    e = lax.axis_index("expert")
    x = dp // NY
    y = lax.rem(dp, NY)

    def zdev(p):
        return (dp, p)

    def xdev(p):
        return (p * NY + y, e)

    def ydev(p):
        return (x * NY + p, e)

    def z_each(make):
        def one(k, c):
            make(lax.rem(e + k, NE))
            return c

        lax.fori_loop(1, NE, one, 0)

    def x_each(make):
        for k in range(1, NX):
            make(lax.rem(x + k, NX))

    def y_each(make):
        for k in range(1, NY):
            make(lax.rem(y + k, NY))

    loads = [
        pltpu.make_async_copy(cot_h, cot, lsem.at[0]),
        pltpu.make_async_copy(aout_h, aout, lsem.at[2]),
        pltpu.make_async_copy(hid_h, hx.at[x], lsem.at[1]),
        pltpu.make_async_copy(ain_h, ain, lsem.at[3]),
        pltpu.make_async_copy(w_h, wm, lsem.at[4]),
    ]
    for one in loads:
        one.start()

    barrier = pltpu.get_barrier_semaphore()
    z_each(lambda p: pl.semaphore_signal(barrier, inc=1, device_id=zdev(p), device_id_type=MESH))
    x_each(lambda p: pl.semaphore_signal(barrier, inc=1, device_id=xdev(p), device_id_type=MESH))
    y_each(lambda p: pl.semaphore_signal(barrier, inc=1, device_id=ydev(p), device_id_type=MESH))

    place = lax.broadcasted_iota(jnp.int32, (NE, CAP, RANK), 1)
    lane = lax.broadcasted_iota(jnp.int32, (NE, CAP, RANK), 2)

    routes = routes_ref[...]
    probs = probs_ref[...].astype(F32)
    expert_id = lax.broadcasted_iota(jnp.int32, (NE, TOK), 0)
    named = jnp.zeros((NE, TOK), F32)
    weight = jnp.zeros((NE, TOK), F32)
    for k in range(8):
        hit = (routes[k : k + 1, :] == expert_id).astype(F32)
        named = named + hit
        weight = weight + hit * probs[k : k + 1, :]
    row = lax.broadcasted_iota(jnp.int32, (TOK, TOK), 0)
    col = lax.broadcasted_iota(jnp.int32, (TOK, TOK), 1)
    before = dot(named.astype(BF16), (row < col).astype(F32).astype(BF16))
    before = jnp.where(named > 0.5, before, -1.0)
    pick3 = (jnp.broadcast_to(before[:, None, :], (NE, CAP, TOK)) == place.astype(F32)).astype(F32)
    pickw = (pick3 * weight[:, None, :]).reshape(SLOTS, TOK)
    sel[...] = pick3.reshape(SLOTS, TOK)
    second = (loop_ref[...] == 1).astype(F32)
    w1 = jnp.sum(pickw * second, axis=1, keepdims=True)
    w0 = jnp.sum(pickw * (1.0 - second), axis=1, keepdims=True)

    def to_rows(column):
        return jnp.broadcast_to(column, (SLOTS, RANK)).reshape(NE, CAP, RANK)

    both = jnp.where(lane == place, to_rows(w0), 0.0) + jnp.where(
        lane == place + CAP, to_rows(w1), 0.0
    )
    mrow[...] = jnp.sum(both, axis=1)[:, None, :]

    def block_of(j):
        off, start, width = STEPS[j]
        return lax.rem(y + off, NY), start, width

    def fill(j):
        yj, start, width = block_of(j)
        picked = sel[...].astype(BF16)

        def one(q, c):
            at = pl.multiple_of((NY * q + yj) * ROWS + start, 128)
            dys[j][q] = dot(picked, cot[:, pl.ds(at, width)]).astype(BF16)
            return c

        lax.fori_loop(0, NX, one, 0)
        dyr[j][:, blk(e), :] = dys[j][:, blk(e), :]

    most = pl.ds(0, (NE - 1) * CAP)

    def dy_copy(j, p):
        return rcopy(dys[j].at[:, blk(p), :], dyr[j].at[:, blk(e), :], z_s.at[j], z_r.at[j], zdev(p))

    def dy_all(j):
        return rcopy(dys[j].at[:, most, :], dyr[j].at[:, most, :], z_s.at[j], z_r.at[j], zdev(e))

    def pj_copy(p):
        return rcopy(pbuf.at[blk(p), :], precv.at[blk(e), :], z_s.at[NS], z_r.at[NS], zdev(p))

    def pj_all():
        return rcopy(pbuf.at[most, :], precv.at[most, :], z_s.at[NS], z_r.at[NS], zdev(e))

    def zc(n, src, dst, p):
        return rcopy(src.at[p], dst.at[e], z_s.at[NS + n], z_r.at[NS + n], zdev(p))

    def zc_all(n, src, dst):
        part = pl.ds(0, NE - 1)
        return rcopy(src.at[part], dst.at[part], z_s.at[NS + n], z_r.at[NS + n], zdev(e))

    def xc(n, src, dst, p):
        return rcopy(src, dst, x_s.at[n], x_r.at[n], xdev(p))

    def yc(n, src, dst, p):
        return rcopy(src, dst, y_s.at[n], y_r.at[n], ydev(p))

    three = pl.ds(0, 3)

    def h_all():
        return xc(0, hx.at[three], hx.at[three], x)

    def m_all():
        return xc(1, mxr.at[three], mxr.at[three], x)

    def q1_all():
        return yc(0, q1s.at[three], q1r.at[three], y)

    def q2_all():
        return xc(2, q2s.at[three], q2r.at[three], x)

    def t_all(j):
        return xc(3 + j, tsd[j].at[three], trv[j].at[three], x)

    def p_copy(j, p):
        off, start, width = STEPS[j]
        at = (off - 1, pl.ds(start, width))
        return yc(1 + j, ps.at[at], pr.at[at], p)

    loads[0].wait()
    fill(0)
    loads[1].wait()
    picked = sel[...].astype(BF16)
    p0 = dot(cot[...], aout[0]).astype(BF16)
    p1 = dot(cot[...], aout[1]).astype(BF16)
    pbuf[...] = jnp.where(w1 > 0.0, dot(picked, p1), dot(picked, p0)).astype(BF16)
    precv[blk(e), :] = pbuf[blk(e), :]
    mxr[x, e] = mrow[e]
    fill(1)
    loads[2].wait()
    pl.semaphore_wait(barrier, NE - 1 + 2 * 3)
    z_each(lambda p: rcopy(mrow.at[p], mxr.at[x, e], z_s.at[NS + 1], z_r.at[NS + 1], zdev(p)).start())
    z_each(lambda p: pj_copy(p).start())
    z_each(lambda p: dy_copy(0, p).start())
    x_each(lambda p: xc(0, hx.at[x], hx.at[x], p).start())
    z_each(lambda p: dy_copy(1, p).start())
    for j in range(2, NS):
        fill(j)
        z_each(lambda p: dy_copy(j, p).start())

    loads[3].wait()
    for p in range(NE):
        pair = jnp.concatenate(
            [ain[0, 8 * p : 8 * p + 8, :].astype(F32), ain[1, 8 * p : 8 * p + 8, :].astype(F32)], axis=0
        )
        aperm[16 * p : 16 * p + 16, :] = pair.astype(BF16)
    hid = hx[x]

    def weights(s):
        got = jnp.broadcast_to(mxr[s], (NE, CAP, RANK))
        low = jnp.sum(jnp.where(lane == place, got, 0.0), axis=2, keepdims=True)
        high = jnp.sum(jnp.where(lane == place + CAP, got, 0.0), axis=2, keepdims=True)
        low = jnp.broadcast_to(low, (NE, CAP, RANK)).reshape(SLOTS, RANK)
        high = jnp.broadcast_to(high, (NE, CAP, RANK)).reshape(SLOTS, RANK)
        return low, high

    lane2 = lax.broadcasted_iota(jnp.int32, (SLOTS, EXT), 1)
    odd = jnp.bitwise_and(jnp.right_shift(lane2, 3), 1) == 1

    def kept(low, high):
        picked_w = jnp.where(
            odd, jnp.concatenate([high, high], axis=1), jnp.concatenate([low, low], axis=1)
        )
        return picked_w > 0.0

    part = pl.ds(0, NE - 1)
    rcopy(mrow.at[part], mxr.at[x, part], z_s.at[NS + 1], z_r.at[NS + 1], zdev(e)).wait_recv()
    x_each(lambda p: xc(1, mxr.at[x], mxr.at[x], p).start())
    low, high = weights(x)
    wfull = low + high
    wv[...] = wfull
    keep = kept(low, high)
    pj_all().wait_recv()
    proj = precv[...]
    r_at = lax.broadcasted_iota(jnp.int32, (RANK, EXT), 0)
    n_at = lax.broadcasted_iota(jnp.int32, (RANK, EXT), 1)
    spread = jnp.bitwise_or(
        jnp.left_shift(jnp.right_shift(n_at, 4), 3), jnp.bitwise_and(n_at, 7)
    )
    expand = (spread == r_at).astype(F32).astype(BF16)
    wproj = (wfull * proj.astype(F32)).astype(BF16)
    wpm = jnp.where(keep, dot(wproj, expand), 0.0).astype(BF16)
    projm = jnp.where(keep, dot(proj, expand), 0.0).astype(BF16)
    acc[...] = dot(projm, aperm[...])
    qt = lax.dot_general(hid, wpm, (((0,), (0,)), ((), ())), preferred_element_type=F32)
    for d in range(NX * NY):
        q1s[d % NY, d // NY] = qt[ACOL * d : ACOL * (d + 1), :].astype(BF16)
    y_each(lambda p: yc(0, q1s.at[p], q1r.at[y], p).start())

    def arrive(j):
        yj, start, width = block_of(j)
        dy_all(j).wait_recv()

        def one(q, c):
            wf = wv[...]
            if width > RANK:
                wf = jnp.concatenate([wf, wf], axis=1)
            tsd[j][q] = (dyr[j][q].astype(F32) * wf).T.astype(BF16)
            return c

        lax.fori_loop(0, NX, one, 0)
        x_each(lambda p: xc(3 + j, tsd[j].at[p], trv[j].at[x], p).start())
        if j == 0:
            loads[4].wait()

        def two(q, c):
            at = pl.multiple_of((NY * q + yj) * ROWS + start, 128)
            acc[...] += dot(dyr[j][q], wm[pl.ds(at, width), :])
            return c

        lax.fori_loop(0, NX, two, 0)

    def product(j):
        t_all(j).wait_recv()
        mine = tsd[j][x]
        main = dot(mine, hx[x])
        extra = dot(mine, dx[x])
        for k in range(1, NX):
            s = lax.rem(x + k, NX)
            main = main + dot(trv[j][s], hx[s])
            extra = extra + dot(trv[j][s], dx[s])
        return main, extra

    def reduce_y(j):
        off, start, width = STEPS[j]
        main, extra = product(j)
        ps[off - 1, start : start + width, :HID] = main.astype(BF16)
        ps[off - 1, start : start + width, HID:] = extra.astype(BF16)
        p_copy(j, lax.rem(y + off, NY)).start()

    def finish_block(j):
        off, start, width = STEPS[j]
        main, extra = product(j)
        for i in range(NP):
            if STEPS[i][2] > width or STEPS[i][1] == start:
                if not (STEPS[i][2] > width and start > 0):
                    p_copy(i, y).wait_recv()
        rows = slice(start, start + width)
        for k in range(3):
            main = main + pr[k, rows, :HID].astype(F32)
            extra = extra + pr[k, rows, HID:].astype(F32)
        dw_ref[rows, :] = main
        h = start // width
        gzs[h] = extra.T.astype(BF16).reshape(NE, 16, width)
        z_each(lambda p: zc(4 + h, gzs.at[h], gzr.at[h], p).start())

    q1_all().wait_recv()
    total = q1s[y].astype(F32)
    for k in range(1, NY):
        total = total + q1r[lax.rem(y + k, NY)].astype(F32)
    q2s[...] = total.astype(BF16)
    x_each(lambda p: xc(2, q2s.at[p], q2r.at[x], p).start())

    arrive(0)
    h_all().wait_recv()
    m_all().wait_recv()
    for k in range(NX):
        s = lax.rem(x + k, NX)
        low, high = weights(s)
        dx[s] = jnp.where(kept(low, high), dot_t(hx[s], aperm[...]), 0.0).astype(BF16)
    arrive(1)
    reduce_y(0)
    arrive(2)
    q2_all().wait_recv()
    total = q2s[x].astype(F32)
    for k in range(1, NX):
        total = total + q2r[lax.rem(x + k, NX)].astype(F32)
    padded = jnp.concatenate([total, jnp.zeros((RANK - ACOL, EXT), F32)], axis=0)
    rzs[...] = padded.T.astype(BF16).reshape(NE, 16, RANK)
    z_each(lambda p: zc(2, rzs, rzr, p).start())
    reduce_y(1)
    arrive(3)
    reduce_y(2)
    arrive(4)
    reduce_y(3)
    arrive(5)
    reduce_y(4)
    arrive(6)

    grad = acc[...]
    mixed = jnp.sum(hx[x].astype(F32) * grad, axis=1, keepdims=True)
    xs[...] = jnp.sum(jnp.where(lane == place, to_rows(mixed), 0.0), axis=1)[:, None, :]
    z_each(lambda p: zc(3, xs, xr, p).start())
    hg_ref[...] = (jnp.concatenate([wv[...]] * (HID // RANK), axis=1) * grad).astype(BF16)

    finish_block(5)

    zc_all(2, rzs, rzr).wait_recv()
    rzr[e] = rzs[e]
    total = jnp.sum(rzr[...].astype(F32), axis=0)
    ga_ref[0] = total[:8, :ACOL]
    ga_ref[1] = total[8:, :ACOL]

    finish_block(6)

    zc_all(3, xs, xr).wait_recv()
    xr[e] = xs[e]
    got = jnp.broadcast_to(xr[...], (NE, CAP, RANK))
    column = jnp.sum(jnp.where(lane == place, got, 0.0), axis=2, keepdims=True)
    per_expert = jnp.sum(sel[...].reshape(NE, CAP, TOK) * column, axis=1)
    for k in range(8):
        hit = routes_ref[k : k + 1, :] == expert_id
        cwg_ref[k : k + 1, :] = jnp.sum(jnp.where(hit, per_expert, 0.0), axis=0, keepdims=True)

    rcopy(mrow.at[part], mxr.at[x, part], z_s.at[NS + 1], z_r.at[NS + 1], zdev(e)).wait_send()
    pj_all().wait_send()
    for j in range(NS):
        dy_all(j).wait_send()
        t_all(j).wait_send()
    h_all().wait_send()
    m_all().wait_send()
    q1_all().wait_send()
    q2_all().wait_send()
    zc_all(2, rzs, rzr).wait_send()
    zc_all(3, xs, xr).wait_send()
    for j in range(NP):
        p_copy(j, y).wait_send()

    for h in range(2):
        zc_all(4 + h, gzs.at[h], gzr.at[h]).wait_recv()
        gzr[h, e] = gzs[h, e]
        total = jnp.sum(gzr[h].astype(F32), axis=0)
        half = slice(h * ROWS // 2, (h + 1) * ROWS // 2)
        gb_ref[0, :, half] = total[:8, :]
        gb_ref[1, :, half] = total[8:, :]
    for h in range(2):
        zc_all(4 + h, gzs.at[h], gzr.at[h]).wait_send()


def store_kernel(*refs):
    ins, outs, sem = refs[:5], refs[5:10], refs[10]
    moves = [pltpu.make_async_copy(a, b, sem.at[n]) for n, (a, b) in enumerate(zip(ins, outs))]
    for one in moves:
        one.start()
    for one in moves:
        one.wait()


def on_device(cotangent, hidden, down_matrix, adapter_in, adapter_out, probs, routes, token_loop):
    vmem = pl.BlockSpec(memory_space=pltpu.VMEM)
    anyw = pl.BlockSpec(memory_space=pl.ANY)
    hbm = pl.BlockSpec(memory_space=pltpu.HBM)
    widths = [w for _, _, w in STEPS]
    scratch = [
        pltpu.VMEM((TOK, MODEL), BF16),
        pltpu.VMEM((2, MODEL, RANK), BF16),
        pltpu.VMEM((2, RANK, HID), BF16),
        pltpu.VMEM((MODEL, HID), BF16),
        pltpu.VMEM((NX, SLOTS, HID), BF16),
        pltpu.VMEM((NX, SLOTS, EXT), BF16),
        pltpu.VMEM((EXT, HID), BF16),
        pltpu.VMEM((SLOTS, RANK), BF16),
        pltpu.VMEM((SLOTS, RANK), BF16),
        pltpu.VMEM((SLOTS, RANK), F32),
        pltpu.VMEM((SLOTS, HID), F32),
        pltpu.VMEM((SLOTS, TOK), F32),
        pltpu.VMEM((NE, 1, RANK), F32),
        pltpu.VMEM((NX, NE, 1, RANK), F32),
        pltpu.VMEM((8, RANK), F32),
        pltpu.VMEM((NY, NX, ACOL, EXT), BF16),
        pltpu.VMEM((NY, NX, ACOL, EXT), BF16),
        pltpu.VMEM((NX, ACOL, EXT), BF16),
        pltpu.VMEM((NX, ACOL, EXT), BF16),
        pltpu.VMEM((NE, 16, RANK), BF16),
        pltpu.VMEM((NE, 16, RANK), BF16),
        pltpu.VMEM((NE, 1, RANK), F32),
        pltpu.VMEM((NE, 1, RANK), F32),
        pltpu.VMEM((2, NE, 16, ROWS // 2), BF16),
        pltpu.VMEM((2, NE, 16, ROWS // 2), BF16),
        pltpu.VMEM((3, ROWS, HID + EXT), BF16),
        pltpu.VMEM((3, ROWS, HID + EXT), BF16),
    ]
    scratch += [pltpu.VMEM((NX, SLOTS, w), BF16) for w in widths]
    scratch += [pltpu.VMEM((NX, SLOTS, w), BF16) for w in widths]
    scratch += [pltpu.VMEM((NX, w, SLOTS), BF16) for w in widths]
    scratch += [pltpu.VMEM((NX, w, SLOTS), BF16) for w in widths]
    sem = pltpu.SemaphoreType.DMA
    scratch += [
        sem((5,)),
        sem((NS + 6,)),
        sem((NS + 6,)),
        sem((3 + NS,)),
        sem((3 + NS,)),
        sem((1 + NP,)),
        sem((1 + NP,)),
    ]
    shapes = (
        ((SLOTS, HID), BF16),
        ((ROWS, HID), F32),
        ((8, TOK), F32),
        ((2, 8, ACOL), F32),
        ((2, 8, ROWS), F32),
    )
    outs = pl.pallas_call(
        kernel,
        out_shape=tuple(pltpu.VMEM(s, t) for s, t in shapes),
        in_specs=[hbm] * 5 + [vmem] * 3,
        out_specs=(vmem,) * 5,
        scratch_shapes=scratch,
        compiler_params=pltpu.CompilerParams(
            collective_id=0, has_side_effects=True, vmem_limit_bytes=56 * 2**20
        ),
        name="backward",
    )(
        cotangent,
        hidden.reshape(SLOTS, HID),
        down_matrix.reshape(MODEL, HID),
        adapter_in,
        adapter_out,
        probs.T,
        routes.T,
        token_loop.reshape(1, TOK),
    )
    hg, dw, cwg, ga, gb = pl.pallas_call(
        store_kernel,
        out_shape=tuple(jax.ShapeDtypeStruct(s, t) for s, t in shapes),
        in_specs=[vmem] * 5,
        out_specs=(anyw,) * 5,
        scratch_shapes=[sem((5,))],
        compiler_params=pltpu.CompilerParams(vmem_limit_bytes=4 * 2**20),
        name="store",
    )(*outs)
    return (
        hg.reshape(hidden.shape),
        dw.reshape(1, ROWS, HID),
        cwg.T,
        ga,
        jnp.swapaxes(gb, 1, 2),
    )


def solution(mesh):
    return jax.shard_map(
        on_device,
        mesh=mesh,
        in_specs=(
            P(("dp", "expert"), None),
            P("dp", "expert", None, None),
            P("expert", None, None),
            P(),
            P(),
            P(("dp", "expert"), None),
            P(("dp", "expert"), None),
            P(("dp", "expert")),
        ),
        out_specs=(
            P("dp", "expert", None, None),
            P("expert", "dp", None),
            P(("dp", "expert"), None),
            P(None, "expert", "dp"),
            P(None, "dp", "expert"),
        ),
        check_vma=False,
    )
```

time: 102 us -> 74.5 us (0.73)
  Pallas kernels: 92.8 us -> 73.7 us
  local copies, waits for them, and re-layouts: 7.72 us -> 0 us
    pallas_call x1 -> x2, Pallas kernels: 92.8 us -> 73.7 us  [the longest x1 72.7 us: on_device(): pl.pallas_call(kernel, out_shape=tuple((pltpu.VMEM(s, t) for s, t in shap...]
    unnamed x5 -> x0, local copies, waits for them, and re-layouts: 7.72 us -> none
where the time goes in v2:
time: 74.5 us; the launch traced here: 74.4 us
  Pallas kernels  73.7 us (99%)
    pallas_call x1, Pallas kernels, on_device(): pl.pallas_call(kernel, out_shape=tuple((pltpu.VMEM(s, t) for s, t in shap...  72.7 us

profile of v2, /device:TPU:1, one launch (start us, length us, event | category | flops | bytes accessed | tf_op | source)
XLA Modules:
  0.0 74.4 jit_solution(8917032487211740033)
XLA Ops:
  0.6 72.7 %backward.1 = (bf16[256,768]{1,0:T(8,128)(2,1)S(1)}, f32[256,768]{1,0:T(8,128)S(1)}, f32[8,128]{1,0:T(8,128)S(1)}, f32[2,8,48]{2,1,0:T(8,128)S(1)}, f32[2,8,256]{2,1,0:T(8,128)S(1)}) custom-call(bf16[128,4096]{1,0:T(8,128)(2,1)} %cot_h.1, bf16[256,768]{1,0:T(8,128)(2,1)} %bitcast.10, bf16[4096,768]{1,0:T(8,128)(2,1)} %bitcast.9, bf16[2,128,768]{2,1,0:T(8,128)(2,1)} %ain_h.1, ...), custom_call_target="tpu_custom_call" | custom-call | tf_op jit(solution)/shard_map/backward/pallas_call | solution.py:482
  73.3 1.1 %store.1 = (bf16[256,768]{1,0:T(8,128)(2,1)}, f32[256,768]{1,0:T(8,128)}, f32[8,128]{1,0:T(8,128)}, f32[2,8,48]{2,1,0:T(8,128)}, f32[2,8,256]{2,1,0:T(8,128)}) custom-call(bf16[256,768]{1,0:T(8,128)(2,1)S(1)} %get-tuple-element.15.refs_0_, f32[256,768]{1,0:T(8,128)S(1)} %get-tuple-element.16.refs_1_, f32[8,128]{1,0:T(8,128)S(1)} %get-tuple-element.17.refs_2_, ...), custom_call_target="tpu_custom_call" | custom-call | tf_op jit(solution)/shard_map/store/pallas_call | solution.py:502

commit v3 on v2

--- a/solution.py
+++ b/solution.py
@@ -24,17 +24,23 @@
 ROWS = MODEL // (NX * NY)
 ACOL = HID // (NX * NY)
 
+ALL = (4, 1, 1)
 STEPS = (
-    (1, 0, 256),
-    (2, 0, 128),
-    (2, 128, 128),
-    (3, 0, 128),
-    (3, 128, 128),
-    (0, 0, 128),
-    (0, 128, 128),
+    (2, ALL, 0, 128),
+    (2, ALL, 128, 128),
+    (1, ALL, 0, 128),
+    (3, ALL, 0, 128),
+    (1, ALL, 128, 128),
+    (3, ALL, 128, 128),
+    (0, (3, 1, 1), 0, 128),
+    (0, (1, 0, 2), 128, 128),
+    (0, (2, 2, 1), 128, 128),
+    (0, (1, 0, 0), 0, 128),
+    (0, (1, 0, 0), 128, 128),
 )
 NS = len(STEPS)
-NP = sum(1 for off, _, _ in STEPS if off)
+NP = sum(1 for step in STEPS if step[0])
+HALF = ROWS // 2
 
 
 def rcopy(src, dst, send, recv, dev):
@@ -51,13 +57,25 @@
     return lax.dot_general(a, b, (((1,), (1,)), ((), ())), preferred_element_type=F32)
 
 
+def owner_offset(j, q):
+    _, a, b = STEPS[j][1]
+    return (a * q + b) % NX
+
+
+def sent_blocks(j):
+    count = STEPS[j][1][0]
+    return sum(1 for q in range(count) if owner_offset(j, q))
+
+
 def blk(p):
     return pl.ds(pl.multiple_of(p * CAP, CAP), CAP)
 
 
-def kernel(cot_h, hid_h, w_h, ain_h, aout_h, probs_ref, routes_ref, loop_ref, *refs):
+def kernel(cot_h, hid_h, w_h, ain_h, aout_h, probs_h, routes_h, loop_h, *refs):
     hg_ref, dw_ref, cwg_ref, ga_ref, gb_ref = refs[:5]
     (cot, aout, ain, wm, hx, dx, aperm, pbuf, precv, wv, acc, sel) = refs[5:17]
+    probs_ref, routes_ref, loop_ref = refs[17:20]
+    refs = refs[3:]
     (mrow, mxr, mxs, q1s, q1r, q2s, q2r, rzs, rzr, xs, xr, gzs, gzr, ps, pr) = refs[17:32]
     dys = refs[32 : 32 + NS]
     dyr = refs[32 + NS : 32 + 2 * NS]
@@ -94,6 +112,16 @@
         for k in range(1, NY):
             make(lax.rem(y + k, NY))
 
+    barrier = pltpu.get_barrier_semaphore()
+    z_each(lambda p: pl.semaphore_signal(barrier, inc=1, device_id=zdev(p), device_id_type=MESH))
+    x_each(lambda p: pl.semaphore_signal(barrier, inc=1, device_id=xdev(p), device_id_type=MESH))
+    y_each(lambda p: pl.semaphore_signal(barrier, inc=1, device_id=ydev(p), device_id_type=MESH))
+
+    small = [
+        pltpu.make_async_copy(routes_h, routes_ref, lsem.at[5]),
+        pltpu.make_async_copy(probs_h, probs_ref, lsem.at[6]),
+        pltpu.make_async_copy(loop_h, loop_ref, lsem.at[7]),
+    ]
     loads = [
         pltpu.make_async_copy(cot_h, cot, lsem.at[0]),
         pltpu.make_async_copy(aout_h, aout, lsem.at[2]),
@@ -101,13 +129,10 @@
         pltpu.make_async_copy(ain_h, ain, lsem.at[3]),
         pltpu.make_async_copy(w_h, wm, lsem.at[4]),
     ]
-    for one in loads:
+    for one in small + loads:
         one.start()
-
-    barrier = pltpu.get_barrier_semaphore()
-    z_each(lambda p: pl.semaphore_signal(barrier, inc=1, device_id=zdev(p), device_id_type=MESH))
-    x_each(lambda p: pl.semaphore_signal(barrier, inc=1, device_id=xdev(p), device_id_type=MESH))
-    y_each(lambda p: pl.semaphore_signal(barrier, inc=1, device_id=ydev(p), device_id_type=MESH))
+    for one in small:
+        one.wait()
 
     place = lax.broadcasted_iota(jnp.int32, (NE, CAP, RANK), 1)
     lane = lax.broadcasted_iota(jnp.int32, (NE, CAP, RANK), 2)
@@ -140,20 +165,19 @@
     )
     mrow[...] = jnp.sum(both, axis=1)[:, None, :]
 
-    def block_of(j):
-        off, start, width = STEPS[j]
-        return lax.rem(y + off, NY), start, width
+    def column(j, q):
+        off, (_, a, b), start, _ = STEPS[j]
+        owner = NY * lax.rem(x + a * q + b, NX) + lax.rem(y + off, NY)
+        return pl.multiple_of(owner * ROWS + start, 128)
 
     def fill(j):
-        yj, start, width = block_of(j)
         picked = sel[...].astype(BF16)
 
         def one(q, c):
-            at = pl.multiple_of((NY * q + yj) * ROWS + start, 128)
-            dys[j][q] = dot(picked, cot[:, pl.ds(at, width)]).astype(BF16)
+            dys[j][q] = dot(picked, cot[:, pl.ds(column(j, q), STEPS[j][3])]).astype(BF16)
             return c
 
-        lax.fori_loop(0, NX, one, 0)
+        lax.fori_loop(0, STEPS[j][1][0], one, 0)
         dyr[j][:, blk(e), :] = dys[j][:, blk(e), :]
 
     most = pl.ds(0, (NE - 1) * CAP)
@@ -197,11 +221,15 @@
     def q2_all():
         return xc(2, q2s.at[three], q2r.at[three], x)
 
+    def t_copy(j, q):
+        return xc(3 + j, tsd[j].at[q], trv[j].at[q], lax.rem(x + owner_offset(j, q), NX))
+
     def t_all(j):
-        return xc(3 + j, tsd[j].at[three], trv[j].at[three], x)
+        part = pl.ds(0, sent_blocks(j))
+        return xc(3 + j, tsd[j].at[part], trv[j].at[part], x)
 
     def p_copy(j, p):
-        off, start, width = STEPS[j]
+        off, _, start, width = STEPS[j]
         at = (off - 1, pl.ds(start, width))
         return yc(1 + j, ps.at[at], pr.at[at], p)
 
@@ -215,6 +243,7 @@
     precv[blk(e), :] = pbuf[blk(e), :]
     mxr[x, e] = mrow[e]
     fill(1)
+    fill(2)
     loads[2].wait()
     pl.semaphore_wait(barrier, NE - 1 + 2 * 3)
     z_each(lambda p: rcopy(mrow.at[p], mxr.at[x, e], z_s.at[NS + 1], z_r.at[NS + 1], zdev(p)).start())
@@ -222,7 +251,8 @@
     z_each(lambda p: dy_copy(0, p).start())
     x_each(lambda p: xc(0, hx.at[x], hx.at[x], p).start())
     z_each(lambda p: dy_copy(1, p).start())
-    for j in range(2, NS):
+    z_each(lambda p: dy_copy(2, p).start())
+    for j in range(3, NS):
         fill(j)
         z_each(lambda p: dy_copy(j, p).start())
 
@@ -276,110 +306,112 @@
     y_each(lambda p: yc(0, q1s.at[p], q1r.at[y], p).start())
 
     def arrive(j):
-        yj, start, width = block_of(j)
+        count, width = STEPS[j][1][0], STEPS[j][3]
         dy_all(j).wait_recv()
 
         def one(q, c):
-            wf = wv[...]
-            if width > RANK:
-                wf = jnp.concatenate([wf, wf], axis=1)
-            tsd[j][q] = (dyr[j][q].astype(F32) * wf).T.astype(BF16)
+            tsd[j][q] = (dyr[j][q].astype(F32) * wv[...]).T.astype(BF16)
             return c
 
-        lax.fori_loop(0, NX, one, 0)
-        x_each(lambda p: xc(3 + j, tsd[j].at[p], trv[j].at[x], p).start())
+        lax.fori_loop(0, count, one, 0)
+        for q in range(sent_blocks(j)):
+            t_copy(j, q).start()
         if j == 0:
             loads[4].wait()
 
         def two(q, c):
-            at = pl.multiple_of((NY * q + yj) * ROWS + start, 128)
-            acc[...] += dot(dyr[j][q], wm[pl.ds(at, width), :])
+            acc[...] += dot(dyr[j][q], wm[pl.ds(column(j, q), width), :])
             return c
 
-        lax.fori_loop(0, NX, two, 0)
-
-    def product(j):
-        t_all(j).wait_recv()
-        mine = tsd[j][x]
-        main = dot(mine, hx[x])
-        extra = dot(mine, dx[x])
-        for k in range(1, NX):
-            s = lax.rem(x + k, NX)
-            main = main + dot(trv[j][s], hx[s])
-            extra = extra + dot(trv[j][s], dx[s])
-        return main, extra
+        lax.fori_loop(0, count, two, 0)
+
+    def product(j, sums=None):
+        if sent_blocks(j):
+            t_all(j).wait_recv()
+        for q in range(STEPS[j][1][0]):
+            back = owner_offset(j, q)
+            block = trv[j][q] if back else tsd[j][q]
+            s = lax.rem(x + NX - back, NX)
+            main, extra = dot(block, hx[s]), dot(block, dx[s])
+            sums = (main, extra) if sums is None else (sums[0] + main, sums[1] + extra)
+        return sums
 
     def reduce_y(j):
-        off, start, width = STEPS[j]
+        off, _, start, width = STEPS[j]
         main, extra = product(j)
         ps[off - 1, start : start + width, :HID] = main.astype(BF16)
         ps[off - 1, start : start + width, HID:] = extra.astype(BF16)
         p_copy(j, lax.rem(y + off, NY)).start()
 
-    def finish_block(j):
-        off, start, width = STEPS[j]
-        main, extra = product(j)
-        for i in range(NP):
-            if STEPS[i][2] > width or STEPS[i][1] == start:
-                if not (STEPS[i][2] > width and start > 0):
-                    p_copy(i, y).wait_recv()
-        rows = slice(start, start + width)
+    def finish_half(h):
+        start = h * HALF
+        sums = None
+        for j in range(NS):
+            if STEPS[j][0] == 0 and STEPS[j][2] == start:
+                sums = product(j, sums)
+        main, extra = sums
+        for j in range(NP):
+            if STEPS[j][2] == start:
+                p_copy(j, y).wait_recv()
+        rows = slice(start, start + HALF)
         for k in range(3):
             main = main + pr[k, rows, :HID].astype(F32)
             extra = extra + pr[k, rows, HID:].astype(F32)
+        gzs[h] = extra.T.astype(BF16).reshape(NE, 16, HALF)
+        z_each(lambda p: zc(4 + h, gzs.at[h], gzr.at[h], p).start())
         dw_ref[rows, :] = main
-        h = start // width
-        gzs[h] = extra.T.astype(BF16).reshape(NE, 16, width)
-        z_each(lambda p: zc(4 + h, gzs.at[h], gzr.at[h], p).start())
-
+
+    arrive(0)
     q1_all().wait_recv()
     total = q1s[y].astype(F32)
     for k in range(1, NY):
         total = total + q1r[lax.rem(y + k, NY)].astype(F32)
     q2s[...] = total.astype(BF16)
     x_each(lambda p: xc(2, q2s.at[p], q2r.at[x], p).start())
-
-    arrive(0)
+    arrive(1)
+    arrive(2)
     h_all().wait_recv()
     m_all().wait_recv()
     for k in range(NX):
         s = lax.rem(x + k, NX)
         low, high = weights(s)
         dx[s] = jnp.where(kept(low, high), dot_t(hx[s], aperm[...]), 0.0).astype(BF16)
-    arrive(1)
     reduce_y(0)
-    arrive(2)
+    reduce_y(1)
+    arrive(3)
     q2_all().wait_recv()
     total = q2s[x].astype(F32)
     for k in range(1, NX):
         total = total + q2r[lax.rem(x + k, NX)].astype(F32)
     padded = jnp.concatenate([total, jnp.zeros((RANK - ACOL, EXT), F32)], axis=0)
-    rzs[...] = padded.T.astype(BF16).reshape(NE, 16, RANK)
+    halves = padded.T.reshape(NE, 2, 8, RANK)
+    rzs[...] = (halves[:, 0] + pltpu.roll(halves[:, 1], ACOL, 2)).astype(BF16)
     z_each(lambda p: zc(2, rzs, rzr, p).start())
-    reduce_y(1)
-    arrive(3)
     reduce_y(2)
     arrive(4)
     reduce_y(3)
     arrive(5)
     reduce_y(4)
     arrive(6)
+    reduce_y(5)
+    arrive(7)
+    arrive(8)
+    arrive(9)
+    finish_half(0)
+    arrive(10)
 
     grad = acc[...]
     mixed = jnp.sum(hx[x].astype(F32) * grad, axis=1, keepdims=True)
     xs[...] = jnp.sum(jnp.where(lane == place, to_rows(mixed), 0.0), axis=1)[:, None, :]
     z_each(lambda p: zc(3, xs, xr, p).start())
-    hg_ref[...] = (jnp.concatenate([wv[...]] * (HID // RANK), axis=1) * grad).astype(BF16)
-
-    finish_block(5)
+    finish_half(1)
+    hg_ref[...] = (jnp.concatenate([wv[...]] * (HID // RANK), axis=1) * acc[...]).astype(BF16)
 
     zc_all(2, rzs, rzr).wait_recv()
     rzr[e] = rzs[e]
     total = jnp.sum(rzr[...].astype(F32), axis=0)
-    ga_ref[0] = total[:8, :ACOL]
-    ga_ref[1] = total[8:, :ACOL]
-
-    finish_block(6)
+    ga_ref[0] = total[:, :ACOL]
+    ga_ref[1] = total[:, ACOL : 2 * ACOL]
 
     zc_all(3, xs, xr).wait_recv()
     xr[e] = xs[e]
@@ -394,7 +426,8 @@
     pj_all().wait_send()
     for j in range(NS):
         dy_all(j).wait_send()
-        t_all(j).wait_send()
+        if sent_blocks(j):
+            t_all(j).wait_send()
     h_all().wait_send()
     m_all().wait_send()
     q1_all().wait_send()
@@ -428,7 +461,7 @@
     vmem = pl.BlockSpec(memory_space=pltpu.VMEM)
     anyw = pl.BlockSpec(memory_space=pl.ANY)
     hbm = pl.BlockSpec(memory_space=pltpu.HBM)
-    widths = [w for _, _, w in STEPS]
+    dims = [(blocks[0], width) for _, blocks, _, width in STEPS]
     scratch = [
         pltpu.VMEM((TOK, MODEL), BF16),
         pltpu.VMEM((2, MODEL, RANK), BF16),
@@ -442,6 +475,9 @@
         pltpu.VMEM((SLOTS, RANK), F32),
         pltpu.VMEM((SLOTS, HID), F32),
         pltpu.VMEM((SLOTS, TOK), F32),
+        pltpu.VMEM((8, TOK), BF16),
+        pltpu.VMEM((8, TOK), jnp.int32),
+        pltpu.VMEM((1, TOK), jnp.int32),
         pltpu.VMEM((NE, 1, RANK), F32),
         pltpu.VMEM((NX, NE, 1, RANK), F32),
         pltpu.VMEM((8, RANK), F32),
@@ -449,8 +485,8 @@
         pltpu.VMEM((NY, NX, ACOL, EXT), BF16),
         pltpu.VMEM((NX, ACOL, EXT), BF16),
         pltpu.VMEM((NX, ACOL, EXT), BF16),
-        pltpu.VMEM((NE, 16, RANK), BF16),
-        pltpu.VMEM((NE, 16, RANK), BF16),
+        pltpu.VMEM((NE, 8, RANK), BF16),
+        pltpu.VMEM((NE, 8, RANK), BF16),
         pltpu.VMEM((NE, 1, RANK), F32),
         pltpu.VMEM((NE, 1, RANK), F32),
         pltpu.VMEM((2, NE, 16, ROWS // 2), BF16),
@@ -458,13 +494,13 @@
         pltpu.VMEM((3, ROWS, HID + EXT), BF16),
         pltpu.VMEM((3, ROWS, HID + EXT), BF16),
     ]
-    scratch += [pltpu.VMEM((NX, SLOTS, w), BF16) for w in widths]
-    scratch += [pltpu.VMEM((NX, SLOTS, w), BF16) for w in widths]
-    scratch += [pltpu.VMEM((NX, w, SLOTS), BF16) for w in widths]
-    scratch += [pltpu.VMEM((NX, w, SLOTS), BF16) for w in widths]
+    scratch += [pltpu.VMEM((n, SLOTS, w), BF16) for n, w in dims]
+    scratch += [pltpu.VMEM((n, SLOTS, w), BF16) for n, w in dims]
+    scratch += [pltpu.VMEM((n, w, SLOTS), BF16) for n, w in dims]
+    scratch += [pltpu.VMEM((n, w, SLOTS), BF16) for n, w in dims]
     sem = pltpu.SemaphoreType.DMA
     scratch += [
-        sem((5,)),
+        sem((8,)),
         sem((NS + 6,)),
         sem((NS + 6,)),
         sem((3 + NS,)),
@@ -482,7 +518,7 @@
     outs = pl.pallas_call(
         kernel,
         out_shape=tuple(pltpu.VMEM(s, t) for s, t in shapes),
-        in_specs=[hbm] * 5 + [vmem] * 3,
+        in_specs=[hbm] * 8,
         out_specs=(vmem,) * 5,
         scratch_shapes=scratch,
         compiler_params=pltpu.CompilerParams(

time: 74.5 us -> 71.5 us (0.960)
  Pallas kernels: 73.7 us -> 70.7 us
    pallas_call x1, Pallas kernels: 72.7 us -> 69.7 us  [on_device(): pl.pallas_call(kernel, out_shape=tuple((pltpu.VMEM(s, t) for s, t in shap...]
where the time goes in v3:
time: 71.5 us; the launch traced here: 71.4 us
  Pallas kernels  70.7 us (99%)
    pallas_call x1, Pallas kernels, on_device(): pl.pallas_call(kernel, out_shape=tuple((pltpu.VMEM(s, t) for s, t in shap...  69.7 us

profile of v3, /device:TPU:1, one launch (start us, length us, event | category | flops | bytes accessed | tf_op | source)
XLA Modules:
  0.0 71.4 jit_solution(6902306882754916529)
XLA Ops:
  0.6 69.7 %backward.1 = (bf16[256,768]{1,0:T(8,128)(2,1)S(1)}, f32[256,768]{1,0:T(8,128)S(1)}, f32[8,128]{1,0:T(8,128)S(1)}, f32[2,8,48]{2,1,0:T(8,128)S(1)}, f32[2,8,256]{2,1,0:T(8,128)S(1)}) custom-call(bf16[128,4096]{1,0:T(8,128)(2,1)} %cot_h.1, bf16[256,768]{1,0:T(8,128)(2,1)} %bitcast.10, bf16[4096,768]{1,0:T(8,128)(2,1)} %bitcast.9, bf16[2,128,768]{2,1,0:T(8,128)(2,1)} %ain_h.1, ...), custom_call_target="tpu_custom_call" | custom-call | tf_op jit(solution)/shard_map/backward/pallas_call | solution.py:518
  70.3 1.1 %store.1 = (bf16[256,768]{1,0:T(8,128)(2,1)}, f32[256,768]{1,0:T(8,128)}, f32[8,128]{1,0:T(8,128)}, f32[2,8,48]{2,1,0:T(8,128)}, f32[2,8,256]{2,1,0:T(8,128)}) custom-call(bf16[256,768]{1,0:T(8,128)(2,1)S(1)} %get-tuple-element.15.refs_0_, f32[256,768]{1,0:T(8,128)S(1)} %get-tuple-element.16.refs_1_, f32[8,128]{1,0:T(8,128)S(1)} %get-tuple-element.17.refs_2_, ...), custom_call_target="tpu_custom_call" | custom-call | tf_op jit(solution)/shard_map/store/pallas_call | solution.py:538

commit v4 on v3

--- a/solution.py
+++ b/solution.py
@@ -31,7 +31,9 @@
     (1, ALL, 0, 128),
     (3, ALL, 0, 128),
     (1, ALL, 128, 128),
-    (3, ALL, 128, 128),
+    (3, (1, 0, 2), 128, 128),
+    (3, (2, 2, 1), 128, 128),
+    (3, (1, 0, 0), 128, 128),
     (0, (3, 1, 1), 0, 128),
     (0, (1, 0, 2), 128, 128),
     (0, (2, 2, 1), 128, 128),
@@ -39,8 +41,9 @@
     (0, (1, 0, 0), 128, 128),
 )
 NS = len(STEPS)
-NP = sum(1 for step in STEPS if step[0])
 HALF = ROWS // 2
+PARTS = ((2, 0), (2, 128), (1, 0), (3, 0), (1, 128), (3, 128))
+NP = len(PARTS)
 
 
 def rcopy(src, dst, send, recv, dev):
@@ -74,8 +77,8 @@
 def kernel(cot_h, hid_h, w_h, ain_h, aout_h, probs_h, routes_h, loop_h, *refs):
     hg_ref, dw_ref, cwg_ref, ga_ref, gb_ref = refs[:5]
     (cot, aout, ain, wm, hx, dx, aperm, pbuf, precv, wv, acc, sel) = refs[5:17]
-    probs_ref, routes_ref, loop_ref = refs[17:20]
-    refs = refs[3:]
+    probs_ref, routes_ref, loop_ref, gsum = refs[17:21]
+    refs = refs[4:]
     (mrow, mxr, mxs, q1s, q1r, q2s, q2r, rzs, rzr, xs, xr, gzs, gzr, ps, pr) = refs[17:32]
     dys = refs[32 : 32 + NS]
     dyr = refs[32 + NS : 32 + 2 * NS]
@@ -99,10 +102,11 @@
 
     def z_each(make):
         def one(k, c):
-            make(lax.rem(e + k, NE))
+            side = 1 - 2 * lax.rem(k, 2)
+            make(lax.rem(e + NE // 2 + side * lax.div(k + 1, 2), NE))
             return c
 
-        lax.fori_loop(1, NE, one, 0)
+        lax.fori_loop(0, NE - 1, one, 0)
 
     def x_each(make):
         for k in range(1, NX):
@@ -228,31 +232,27 @@
         part = pl.ds(0, sent_blocks(j))
         return xc(3 + j, tsd[j].at[part], trv[j].at[part], x)
 
-    def p_copy(j, p):
-        off, _, start, width = STEPS[j]
-        at = (off - 1, pl.ds(start, width))
-        return yc(1 + j, ps.at[at], pr.at[at], p)
+    def p_copy(n, p):
+        off, start = PARTS[n]
+        at = (off - 1, pl.ds(start, HALF))
+        return yc(1 + n, ps.at[at], pr.at[at], p)
 
     loads[0].wait()
     fill(0)
+    pl.semaphore_wait(barrier, NE - 1 + 2 * 3)
+    z_each(lambda p: dy_copy(0, p).start())
+    loads[2].wait()
+    x_each(lambda p: xc(0, hx.at[x], hx.at[x], p).start())
+    mxr[x, e] = mrow[e]
+    z_each(lambda p: rcopy(mrow.at[p], mxr.at[x, e], z_s.at[NS + 1], z_r.at[NS + 1], zdev(p)).start())
     loads[1].wait()
     picked = sel[...].astype(BF16)
     p0 = dot(cot[...], aout[0]).astype(BF16)
     p1 = dot(cot[...], aout[1]).astype(BF16)
     pbuf[...] = jnp.where(w1 > 0.0, dot(picked, p1), dot(picked, p0)).astype(BF16)
     precv[blk(e), :] = pbuf[blk(e), :]
-    mxr[x, e] = mrow[e]
-    fill(1)
-    fill(2)
-    loads[2].wait()
-    pl.semaphore_wait(barrier, NE - 1 + 2 * 3)
-    z_each(lambda p: rcopy(mrow.at[p], mxr.at[x, e], z_s.at[NS + 1], z_r.at[NS + 1], zdev(p)).start())
     z_each(lambda p: pj_copy(p).start())
-    z_each(lambda p: dy_copy(0, p).start())
-    x_each(lambda p: xc(0, hx.at[x], hx.at[x], p).start())
-    z_each(lambda p: dy_copy(1, p).start())
-    z_each(lambda p: dy_copy(2, p).start())
-    for j in range(3, NS):
+    for j in range(1, NS):
         fill(j)
         z_each(lambda p: dy_copy(j, p).start())
 
@@ -306,24 +306,26 @@
     y_each(lambda p: yc(0, q1s.at[p], q1r.at[y], p).start())
 
     def arrive(j):
-        count, width = STEPS[j][1][0], STEPS[j][3]
         dy_all(j).wait_recv()
 
         def one(q, c):
             tsd[j][q] = (dyr[j][q].astype(F32) * wv[...]).T.astype(BF16)
             return c
 
-        lax.fori_loop(0, count, one, 0)
+        lax.fori_loop(0, STEPS[j][1][0], one, 0)
         for q in range(sent_blocks(j)):
             t_copy(j, q).start()
         if j == 0:
             loads[4].wait()
-
+        if j < NS - 1:
+            add_grad(j)
+
+    def add_grad(j):
         def two(q, c):
-            acc[...] += dot(dyr[j][q], wm[pl.ds(column(j, q), width), :])
+            acc[...] += dot(dyr[j][q], wm[pl.ds(column(j, q), STEPS[j][3]), :])
             return c
 
-        lax.fori_loop(0, count, two, 0)
+        lax.fori_loop(0, STEPS[j][1][0], two, 0)
 
     def product(j, sums=None):
         if sent_blocks(j):
@@ -336,40 +338,47 @@
             sums = (main, extra) if sums is None else (sums[0] + main, sums[1] + extra)
         return sums
 
-    def reduce_y(j):
-        off, _, start, width = STEPS[j]
-        main, extra = product(j)
-        ps[off - 1, start : start + width, :HID] = main.astype(BF16)
-        ps[off - 1, start : start + width, HID:] = extra.astype(BF16)
-        p_copy(j, lax.rem(y + off, NY)).start()
+    def product_of(off, start, own_first=False):
+        steps = [j for j in range(NS) if STEPS[j][0] == off and STEPS[j][2] == start]
+        if own_first:
+            steps = steps[-1:] + steps[:-1]
+        sums = None
+        for j in steps:
+            sums = product(j, sums)
+        return sums
+
+    def reduce_y(n):
+        off, start = PARTS[n]
+        main, extra = product_of(off, start)
+        ps[off - 1, start : start + HALF, :HID] = main.astype(BF16)
+        ps[off - 1, start : start + HALF, HID:] = extra.astype(BF16)
+        p_copy(n, lax.rem(y + off, NY)).start()
+
+    def gather_y(h):
+        start = h * HALF
+        for n in range(NP):
+            if PARTS[n][1] == start:
+                p_copy(n, y).wait_recv()
+        rows = slice(start, start + HALF)
+        part = pr[0, rows, :].astype(F32) + pr[1, rows, :].astype(F32) + pr[2, rows, :].astype(F32)
+        dw_ref[rows, :] = part[:, :HID]
+        gsum[...] = part[:, HID:]
 
     def finish_half(h):
-        start = h * HALF
-        sums = None
-        for j in range(NS):
-            if STEPS[j][0] == 0 and STEPS[j][2] == start:
-                sums = product(j, sums)
-        main, extra = sums
-        for j in range(NP):
-            if STEPS[j][2] == start:
-                p_copy(j, y).wait_recv()
-        rows = slice(start, start + HALF)
-        for k in range(3):
-            main = main + pr[k, rows, :HID].astype(F32)
-            extra = extra + pr[k, rows, HID:].astype(F32)
-        gzs[h] = extra.T.astype(BF16).reshape(NE, 16, HALF)
+        main, extra = product_of(0, h * HALF, True)
+        rows = slice(h * HALF, (h + 1) * HALF)
+        gzs[h] = (extra + gsum[...]).T.astype(BF16).reshape(NE, 16, HALF)
         z_each(lambda p: zc(4 + h, gzs.at[h], gzr.at[h], p).start())
-        dw_ref[rows, :] = main
+        dw_ref[rows, :] += main
 
     arrive(0)
+    arrive(1)
     q1_all().wait_recv()
     total = q1s[y].astype(F32)
     for k in range(1, NY):
         total = total + q1r[lax.rem(y + k, NY)].astype(F32)
     q2s[...] = total.astype(BF16)
     x_each(lambda p: xc(2, q2s.at[p], q2r.at[x], p).start())
-    arrive(1)
-    arrive(2)
     h_all().wait_recv()
     m_all().wait_recv()
     for k in range(NX):
@@ -377,6 +386,7 @@
         low, high = weights(s)
         dx[s] = jnp.where(kept(low, high), dot_t(hx[s], aperm[...]), 0.0).astype(BF16)
     reduce_y(0)
+    arrive(2)
     reduce_y(1)
     arrive(3)
     q2_all().wait_recv()
@@ -391,17 +401,20 @@
     arrive(4)
     reduce_y(3)
     arrive(5)
+    arrive(6)
     reduce_y(4)
-    arrive(6)
+    arrive(7)
     reduce_y(5)
-    arrive(7)
     arrive(8)
     arrive(9)
+    arrive(10)
+    gather_y(0)
+    arrive(11)
     finish_half(0)
-    arrive(10)
-
-    grad = acc[...]
-    mixed = jnp.sum(hx[x].astype(F32) * grad, axis=1, keepdims=True)
+    gather_y(1)
+    arrive(12)
+    add_grad(12)
+    mixed = jnp.sum(hx[x].astype(F32) * acc[...], axis=1, keepdims=True)
     xs[...] = jnp.sum(jnp.where(lane == place, to_rows(mixed), 0.0), axis=1)[:, None, :]
     z_each(lambda p: zc(3, xs, xr, p).start())
     finish_half(1)
@@ -478,6 +491,7 @@
         pltpu.VMEM((8, TOK), BF16),
         pltpu.VMEM((8, TOK), jnp.int32),
         pltpu.VMEM((1, TOK), jnp.int32),
+        pltpu.VMEM((HALF, EXT), F32),
         pltpu.VMEM((NE, 1, RANK), F32),
         pltpu.VMEM((NX, NE, 1, RANK), F32),
         pltpu.VMEM((8, RANK), F32),

time: 71.5 us -> 68.9 us (0.964)
  Pallas kernels: 70.7 us -> 68.2 us
    pallas_call x1, Pallas kernels: 69.7 us -> 67.1 us  [on_device(): pl.pallas_call(kernel, out_shape=tuple((pltpu.VMEM(s, t) for s, t in shap...]
where the time goes in v4:
time: 68.9 us; the launch traced here: 68.8 us
  Pallas kernels  68.2 us (99%)
    pallas_call x1, Pallas kernels, on_device(): pl.pallas_call(kernel, out_shape=tuple((pltpu.VMEM(s, t) for s, t in shap...  67.1 us

profile of v4, /device:TPU:1, one launch (start us, length us, event | category | flops | bytes accessed | tf_op | source)
XLA Modules:
  0.0 68.8 jit_solution(579931001346735992)
XLA Ops:
  0.6 67.1 %backward.1 = (bf16[256,768]{1,0:T(8,128)(2,1)S(1)}, f32[256,768]{1,0:T(8,128)S(1)}, f32[8,128]{1,0:T(8,128)S(1)}, f32[2,8,48]{2,1,0:T(8,128)S(1)}, f32[2,8,256]{2,1,0:T(8,128)S(1)}) custom-call(bf16[128,4096]{1,0:T(8,128)(2,1)} %cot_h.1, bf16[256,768]{1,0:T(8,128)(2,1)} %bitcast.10, bf16[4096,768]{1,0:T(8,128)(2,1)} %bitcast.9, bf16[2,128,768]{2,1,0:T(8,128)(2,1)} %ain_h.1, ...), custom_call_target="tpu_custom_call" | custom-call | tf_op jit(solution)/shard_map/backward/pallas_call | solution.py:532
  67.8 1.1 %store.1 = (bf16[256,768]{1,0:T(8,128)(2,1)}, f32[256,768]{1,0:T(8,128)}, f32[8,128]{1,0:T(8,128)}, f32[2,8,48]{2,1,0:T(8,128)}, f32[2,8,256]{2,1,0:T(8,128)}) custom-call(bf16[256,768]{1,0:T(8,128)(2,1)S(1)} %get-tuple-element.15.refs_0_, f32[256,768]{1,0:T(8,128)S(1)} %get-tuple-element.16.refs_1_, f32[8,128]{1,0:T(8,128)S(1)} %get-tuple-element.17.refs_2_, ...), custom_call_target="tpu_custom_call" | custom-call | tf_op jit(solution)/shard_map/store/pallas_call | solution.py:552

commit v5 on v4

--- a/solution.py
+++ b/solution.py
@@ -34,8 +34,9 @@
     (3, (1, 0, 2), 128, 128),
     (3, (2, 2, 1), 128, 128),
     (3, (1, 0, 0), 128, 128),
-    (0, (3, 1, 1), 0, 128),
+    (0, (1, 0, 2), 0, 128),
     (0, (1, 0, 2), 128, 128),
+    (0, (2, 2, 1), 0, 128),
     (0, (2, 2, 1), 128, 128),
     (0, (1, 0, 0), 0, 128),
     (0, (1, 0, 0), 128, 128),
@@ -117,7 +118,9 @@
             make(lax.rem(y + k, NY))
 
     barrier = pltpu.get_barrier_semaphore()
-    z_each(lambda p: pl.semaphore_signal(barrier, inc=1, device_id=zdev(p), device_id_type=MESH))
+    for k in range(NE - 1):
+        p = lax.rem(e + NE // 2 + (1 - 2 * (k % 2)) * ((k + 1) // 2), NE)
+        pl.semaphore_signal(barrier, inc=1, device_id=zdev(p), device_id_type=MESH)
     x_each(lambda p: pl.semaphore_signal(barrier, inc=1, device_id=xdev(p), device_id_type=MESH))
     y_each(lambda p: pl.semaphore_signal(barrier, inc=1, device_id=ydev(p), device_id_type=MESH))
 
@@ -155,19 +158,10 @@
     before = dot(named.astype(BF16), (row < col).astype(F32).astype(BF16))
     before = jnp.where(named > 0.5, before, -1.0)
     pick3 = (jnp.broadcast_to(before[:, None, :], (NE, CAP, TOK)) == place.astype(F32)).astype(F32)
-    pickw = (pick3 * weight[:, None, :]).reshape(SLOTS, TOK)
     sel[...] = pick3.reshape(SLOTS, TOK)
-    second = (loop_ref[...] == 1).astype(F32)
-    w1 = jnp.sum(pickw * second, axis=1, keepdims=True)
-    w0 = jnp.sum(pickw * (1.0 - second), axis=1, keepdims=True)
 
     def to_rows(column):
         return jnp.broadcast_to(column, (SLOTS, RANK)).reshape(NE, CAP, RANK)
-
-    both = jnp.where(lane == place, to_rows(w0), 0.0) + jnp.where(
-        lane == place + CAP, to_rows(w1), 0.0
-    )
-    mrow[...] = jnp.sum(both, axis=1)[:, None, :]
 
     def column(j, q):
         off, (_, a, b), start, _ = STEPS[j]
@@ -243,6 +237,14 @@
     z_each(lambda p: dy_copy(0, p).start())
     loads[2].wait()
     x_each(lambda p: xc(0, hx.at[x], hx.at[x], p).start())
+    pickw = (pick3 * weight[:, None, :]).reshape(SLOTS, TOK)
+    second = (loop_ref[...] == 1).astype(F32)
+    w1 = jnp.sum(pickw * second, axis=1, keepdims=True)
+    w0 = jnp.sum(pickw * (1.0 - second), axis=1, keepdims=True)
+    both = jnp.where(lane == place, to_rows(w0), 0.0) + jnp.where(
+        lane == place + CAP, to_rows(w1), 0.0
+    )
+    mrow[...] = jnp.sum(both, axis=1)[:, None, :]
     mxr[x, e] = mrow[e]
     z_each(lambda p: rcopy(mrow.at[p], mxr.at[x, e], z_s.at[NS + 1], z_r.at[NS + 1], zdev(p)).start())
     loads[1].wait()
@@ -327,29 +329,28 @@
 
         lax.fori_loop(0, STEPS[j][1][0], two, 0)
 
-    def product(j, sums=None):
-        if sent_blocks(j):
-            t_all(j).wait_recv()
-        for q in range(STEPS[j][1][0]):
-            back = owner_offset(j, q)
+    def blocks_of(off, start):
+        found = []
+        for j in range(NS):
+            if STEPS[j][0] == off and STEPS[j][2] == start:
+                found += [(j, q, owner_offset(j, q)) for q in range(STEPS[j][1][0])]
+        return sorted(found, key=lambda entry: (entry[2] > 0, entry[0], entry[1]))
+
+    def product(off, start, right, wait):
+        total, seen = None, set()
+        for j, q, back in blocks_of(off, start):
+            if wait and back and j not in seen:
+                t_all(j).wait_recv()
+                seen.add(j)
             block = trv[j][q] if back else tsd[j][q]
-            s = lax.rem(x + NX - back, NX)
-            main, extra = dot(block, hx[s]), dot(block, dx[s])
-            sums = (main, extra) if sums is None else (sums[0] + main, sums[1] + extra)
-        return sums
-
-    def product_of(off, start, own_first=False):
-        steps = [j for j in range(NS) if STEPS[j][0] == off and STEPS[j][2] == start]
-        if own_first:
-            steps = steps[-1:] + steps[:-1]
-        sums = None
-        for j in steps:
-            sums = product(j, sums)
-        return sums
+            term = dot(block, right[lax.rem(x + NX - back, NX)])
+            total = term if total is None else total + term
+        return total
 
     def reduce_y(n):
         off, start = PARTS[n]
-        main, extra = product_of(off, start)
+        main = product(off, start, hx, True)
+        extra = product(off, start, dx, False)
         ps[off - 1, start : start + HALF, :HID] = main.astype(BF16)
         ps[off - 1, start : start + HALF, HID:] = extra.astype(BF16)
         p_copy(n, lax.rem(y + off, NY)).start()
@@ -365,11 +366,13 @@
         gsum[...] = part[:, HID:]
 
     def finish_half(h):
-        main, extra = product_of(0, h * HALF, True)
-        rows = slice(h * HALF, (h + 1) * HALF)
+        extra = product(0, h * HALF, dx, True)
         gzs[h] = (extra + gsum[...]).T.astype(BF16).reshape(NE, 16, HALF)
         z_each(lambda p: zc(4 + h, gzs.at[h], gzr.at[h], p).start())
-        dw_ref[rows, :] += main
+
+    def finish_main(h):
+        rows = slice(h * HALF, (h + 1) * HALF)
+        dw_ref[rows, :] += product(0, h * HALF, hx, False)
 
     arrive(0)
     arrive(1)
@@ -404,20 +407,23 @@
     arrive(6)
     reduce_y(4)
     arrive(7)
+    arrive(8)
     reduce_y(5)
-    arrive(8)
     arrive(9)
     arrive(10)
+    arrive(11)
     gather_y(0)
-    arrive(11)
+    arrive(12)
     finish_half(0)
     gather_y(1)
-    arrive(12)
-    add_grad(12)
+    arrive(13)
+    add_grad(13)
     mixed = jnp.sum(hx[x].astype(F32) * acc[...], axis=1, keepdims=True)
     xs[...] = jnp.sum(jnp.where(lane == place, to_rows(mixed), 0.0), axis=1)[:, None, :]
     z_each(lambda p: zc(3, xs, xr, p).start())
     finish_half(1)
+    finish_main(0)
+    finish_main(1)
     hg_ref[...] = (jnp.concatenate([wv[...]] * (HID // RANK), axis=1) * acc[...]).astype(BF16)
 
     zc_all(2, rzs, rzr).wait_recv()

time: 68.9 us -> 68.7 us (level)
  no operation moved by 1% of the time
where the time goes in v5:
time: 68.7 us; the launch traced here: 68.6 us
  Pallas kernels  67.9 us (99%)
    pallas_call x1, Pallas kernels, on_device(): pl.pallas_call(kernel, out_shape=tuple((pltpu.VMEM(s, t) for s, t in shap...  66.9 us

profile of v5, /device:TPU:1, one launch (start us, length us, event | category | flops | bytes accessed | tf_op | source)
XLA Modules:
  0.0 68.6 jit_solution(10552172015966068686)
XLA Ops:
  0.6 66.9 %backward.1 = (bf16[256,768]{1,0:T(8,128)(2,1)S(1)}, f32[256,768]{1,0:T(8,128)S(1)}, f32[8,128]{1,0:T(8,128)S(1)}, f32[2,8,48]{2,1,0:T(8,128)S(1)}, f32[2,8,256]{2,1,0:T(8,128)S(1)}) custom-call(bf16[128,4096]{1,0:T(8,128)(2,1)} %cot_h.1, bf16[256,768]{1,0:T(8,128)(2,1)} %bitcast.10, bf16[4096,768]{1,0:T(8,128)(2,1)} %bitcast.9, bf16[2,128,768]{2,1,0:T(8,128)(2,1)} %ain_h.1, ...), custom_call_target="tpu_custom_call" | custom-call | tf_op jit(solution)/shard_map/backward/pallas_call | solution.py:538
  67.5 1.1 %store.1 = (bf16[256,768]{1,0:T(8,128)(2,1)}, f32[256,768]{1,0:T(8,128)}, f32[8,128]{1,0:T(8,128)}, f32[2,8,48]{2,1,0:T(8,128)}, f32[2,8,256]{2,1,0:T(8,128)}) custom-call(bf16[256,768]{1,0:T(8,128)(2,1)S(1)} %get-tuple-element.15.refs_0_, f32[256,768]{1,0:T(8,128)S(1)} %get-tuple-element.16.refs_1_, f32[8,128]{1,0:T(8,128)S(1)} %get-tuple-element.17.refs_2_, ...), custom_call_target="tpu_custom_call" | custom-call | tf_op jit(solution)/shard_map/store/pallas_call | solution.py:558

commit v6 on v5

--- a/solution.py
+++ b/solution.py
@@ -310,13 +310,10 @@
     def arrive(j):
         dy_all(j).wait_recv()
 
-        def one(q, c):
+        for q in range(STEPS[j][1][0]):
             tsd[j][q] = (dyr[j][q].astype(F32) * wv[...]).T.astype(BF16)
-            return c
-
-        lax.fori_loop(0, STEPS[j][1][0], one, 0)
-        for q in range(sent_blocks(j)):
-            t_copy(j, q).start()
+            if q < sent_blocks(j):
+                t_copy(j, q).start()
         if j == 0:
             loads[4].wait()
         if j < NS - 1:

time: 68.7 us -> 68.5 us (level)
  no operation moved by 1% of the time
where the time goes in v6:
time: 68.5 us
  Pallas kernels  67.8 us (99%)
    pallas_call x1, Pallas kernels, on_device(): pl.pallas_call(kernel, out_shape=tuple((pltpu.VMEM(s, t) for s, t in shap...  66.8 us

profile of v6, /device:TPU:1, one launch (start us, length us, event | category | flops | bytes accessed | tf_op | source)
XLA Modules:
  0.0 68.5 jit_solution(6356324450433861408)
XLA Ops:
  0.6 66.8 %backward.1 = (bf16[256,768]{1,0:T(8,128)(2,1)S(1)}, f32[256,768]{1,0:T(8,128)S(1)}, f32[8,128]{1,0:T(8,128)S(1)}, f32[2,8,48]{2,1,0:T(8,128)S(1)}, f32[2,8,256]{2,1,0:T(8,128)S(1)}) custom-call(bf16[128,4096]{1,0:T(8,128)(2,1)} %cot_h.1, bf16[256,768]{1,0:T(8,128)(2,1)} %bitcast.10, bf16[4096,768]{1,0:T(8,128)(2,1)} %bitcast.9, bf16[2,128,768]{2,1,0:T(8,128)(2,1)} %ain_h.1, ...), custom_call_target="tpu_custom_call" | custom-call | tf_op jit(solution)/shard_map/backward/pallas_call | solution.py:535
  67.4 1.1 %store.1 = (bf16[256,768]{1,0:T(8,128)(2,1)}, f32[256,768]{1,0:T(8,128)}, f32[8,128]{1,0:T(8,128)}, f32[2,8,48]{2,1,0:T(8,128)}, f32[2,8,256]{2,1,0:T(8,128)}) custom-call(bf16[256,768]{1,0:T(8,128)(2,1)S(1)} %get-tuple-element.15.refs_0_, f32[256,768]{1,0:T(8,128)S(1)} %get-tuple-element.16.refs_1_, f32[8,128]{1,0:T(8,128)S(1)} %get-tuple-element.17.refs_2_, ...), custom_call_target="tpu_custom_call" | custom-call | tf_op jit(solution)/shard_map/store/pallas_call | solution.py:555
